TPU v7x, 128 devices: a whole 4x4x4 slice. The times are simulated.
128 devices in a mesh: exp: 4 (over x), tp: 32 (over z, y, core).
Axes of the slice: x: 4, y: 4, z: 4, core: 2. Of those that a mesh axis runs over, the one named last changes fastest.
Arguments:
- inputs: bfloat16 [1024, 4096], P(('exp', 'tp')), may hold values from -6 to 6
- conv_weight: float32 [4, 4096], replicated, may hold values from -3 to 3
- expert_ids: int32 [1024, 2], P(('exp', 'tp')), may hold values from 0 to 7, all different within a row; in each aligned block of 8 rows (0 to 7, 8 to 15, ...) at most 3 rows name the same one
- gate_values: float32 [1024, 2], P(('exp', 'tp')), may hold values from 0.25 to 1
- cotangent: bfloat16 [1024, 4096], P(('exp', 'tp')), may hold values from -6 to 6
- gate_weight: bfloat16 [8, 4096, 14336], P('exp', None, 'tp'), may hold values from -0.09375 to 0.09375
- up_weight: bfloat16 [8, 4096, 14336], P('exp', None, 'tp'), may hold values from -0.09375 to 0.09375
- down_weight: bfloat16 [8, 14336, 4096], P('exp', 'tp'), may hold values from -0.046875 to 0.046875
Outputs:
- result: bfloat16 [1024, 4096], P(('exp', 'tp'))
- grad_inputs: bfloat16 [1024, 4096], P(('exp', 'tp'))
Inputs may be any that keep to these rules, and one draw needn't show every extreme that they name: `expert_ids`: the experts of one token differ. Among the 8 tokens of one device no expert is named more than 3 times, a bound that some block reaches; every expert is named somewhere.
All inputs are finite; a program needn't handle non-finite values.
Results may differ from a plain program's by a relative error of at most 0.014.
Values may be sent and summed in bfloat16 or wider, within the bound.
A program may use at most 128 MiB of HBM per device.

v0:
```python
import jax
import jax.numpy as jnp
from jax import lax
from jax.sharding import PartitionSpec as P


def shifted(array, axis, by):
    size = lax.axis_size(axis)
    pairs = [(i, i + by) for i in range(size) if 0 <= i + by < size]
    return lax.ppermute(array, axis, pairs)


def expert_rows(rows_in, rows_grad, gate_weight, up_weight, down_weight):
    gate_pre = jnp.einsum(
        "mjsd,jdf->mjsf", rows_in, gate_weight, preferred_element_type=jnp.float32
    )
    up_pre = jnp.einsum("mjsd,jdf->mjsf", rows_in, up_weight, preferred_element_type=jnp.float32)
    sigmoid_gate = jax.nn.sigmoid(gate_pre)
    activated = gate_pre * sigmoid_gate
    hidden = (activated * up_pre).astype(jnp.bfloat16)
    forward_part = jnp.einsum(
        "mjsf,jfd->mjsd", hidden, down_weight, preferred_element_type=jnp.float32
    )
    back_hidden = jnp.einsum(
        "mjsd,jfd->mjsf", rows_grad, down_weight, preferred_element_type=jnp.float32
    )
    grad_gate = (
        back_hidden * up_pre * sigmoid_gate * (1.0 + gate_pre * (1.0 - sigmoid_gate))
    ).astype(jnp.bfloat16)
    grad_up = (back_hidden * activated).astype(jnp.bfloat16)
    backward_part = jnp.einsum(
        "mjsf,jdf->mjsd", grad_gate, gate_weight, preferred_element_type=jnp.float32
    ) + jnp.einsum("mjsf,jdf->mjsd", grad_up, up_weight, preferred_element_type=jnp.float32)
    return (forward_part, backward_part)


def per_device(
    inputs, conv_weight, expert_ids, gate_values, cotangent, gate_weight, up_weight, down_weight
):
    tok_rows = inputs.shape[0]
    model_width = inputs.shape[1]
    kernel = conv_weight.shape[0]
    top_count = expert_ids.shape[1]
    groups = lax.axis_size("exp")
    per_group = gate_weight.shape[0]
    experts = groups * per_group
    slot_count = tok_rows * top_count * 3 // (2 * experts)
    source = inputs.astype(jnp.float32)
    rim_rows = shifted(inputs[tok_rows - (kernel - 1) :], ("exp", "tp"), 1)
    extended = jnp.concatenate([rim_rows.astype(jnp.float32), source], 0)
    conv_sum = source
    for shift_step in range(kernel):
        conv_sum = (
            conv_sum
            + conv_weight[shift_step]
            * extended[kernel - 1 - shift_step : kernel - 1 - shift_step + tok_rows]
        )
    mixed = conv_sum.astype(jnp.bfloat16)
    flat_ids = expert_ids.reshape(-1)
    onehot_ids = (flat_ids[:, None] == jnp.arange(experts, dtype=jnp.int32)[None, :]).astype(
        jnp.int32
    )
    earlier = jnp.cumsum(onehot_ids, 0) - onehot_ids
    slot_index = jnp.sum(earlier * onehot_ids, 1)
    target = flat_ids * slot_count + slot_index
    places = (
        jnp.arange(experts * slot_count, dtype=jnp.int32)[:, None] == target[None, :]
    ).reshape(experts * slot_count, tok_rows, top_count)
    dispatch_map = jnp.any(places, 2).astype(jnp.bfloat16)
    packed_in = (
        jnp.dot(dispatch_map, mixed, preferred_element_type=jnp.float32)
        .astype(jnp.bfloat16)
        .reshape(groups, per_group, slot_count, model_width)
    )
    packed_grad = (
        jnp.dot(dispatch_map, cotangent, preferred_element_type=jnp.float32)
        .astype(jnp.bfloat16)
        .reshape(groups, per_group, slot_count, model_width)
    )
    recv_in, recv_grad = (
        lax.all_to_all(packed_in, "exp", split_axis=0, concat_axis=0, tiled=True),
        lax.all_to_all(packed_grad, "exp", split_axis=0, concat_axis=0, tiled=True),
    )
    stacked = jnp.stack([recv_in, recv_grad], 0)[None]
    piece = lax.all_gather(stacked, "tp", axis=0, tiled=True)
    piece_rows = piece.shape[0]
    rows_in = piece[:, 0].reshape(piece_rows * groups, per_group, slot_count, model_width)
    rows_grad = piece[:, 1].reshape(piece_rows * groups, per_group, slot_count, model_width)
    forward_part, backward_part = expert_rows(
        rows_in, rows_grad, gate_weight, up_weight, down_weight
    )
    shape_back = (piece_rows, groups, per_group, slot_count, model_width)
    partials = jnp.stack(
        [
            forward_part.astype(jnp.bfloat16).reshape(shape_back),
            backward_part.astype(jnp.bfloat16).reshape(shape_back),
        ],
        1,
    )
    summed = lax.psum(partials, "tp").astype(jnp.float32)
    own_sums = lax.dynamic_index_in_dim(summed, lax.axis_index("tp"), 0, keepdims=False)
    returned = lax.all_to_all(
        own_sums.astype(jnp.bfloat16), "exp", split_axis=1, concat_axis=1, tiled=True
    ).astype(own_sums.dtype)
    expert_out = returned[0].reshape(experts * slot_count, model_width)
    expert_back = returned[1].reshape(experts * slot_count, model_width)
    picked_out = jnp.take(expert_out, target, axis=0).reshape(tok_rows, top_count, model_width)
    picked_back = jnp.take(expert_back, target, axis=0).reshape(tok_rows, top_count, model_width)
    moe_out = jnp.sum(picked_out * gate_values[:, :, None], 1)
    moe_back = jnp.sum(picked_back * gate_values[:, :, None], 1)
    result = (mixed.astype(jnp.float32) + moe_out).astype(jnp.bfloat16)
    grad_mixed = cotangent.astype(jnp.float32) + moe_back
    next_rows = shifted(grad_mixed[: kernel - 1].astype(jnp.bfloat16), ("exp", "tp"), -1).astype(
        jnp.float32
    )
    extended_grad = jnp.concatenate([grad_mixed, next_rows], 0)
    grad_sum = grad_mixed
    for shift_step in range(kernel):
        grad_sum = (
            grad_sum + conv_weight[shift_step] * extended_grad[shift_step : shift_step + tok_rows]
        )
    return (result, grad_sum.astype(jnp.bfloat16))


def solution(mesh):
    in_specs = (
        P(("exp", "tp"), None),
        P(),
        P(("exp", "tp"), None),
        P(("exp", "tp"), None),
        P(("exp", "tp"), None),
        P("exp", None, "tp"),
        P("exp", None, "tp"),
        P("exp", "tp", None),
    )
    out_specs = (P(("exp", "tp"), None), P(("exp", "tp"), None))
    return jax.shard_map(
        per_device, mesh=mesh, in_specs=in_specs, out_specs=out_specs, check_vma=False
    )
```

profile of v0, /device:TPU:1, one launch (start us, length us, event | category | flops | bytes accessed | tf_op | source)
XLA Modules:
  0.0 402.5 jit_solution(1930475148583040575)
XLA Ops:
  8.0 4.6 %collective-permute-start = (bf16[3,4096]{1,0:T(4,128)(2,1)S(1)}, bf16[3,4096]{1,0:T(4,128)(2,1)S(1)}, u32[]{:S(2)}, u32[]{:S(2)}) collective-permute-start(bf16[3,4096]{1,0:T(4,128)(2,1)S(1)} %slice.55), channel_id=1, source_target_pairs={{0,1},{1,2},{2,3},{3,4},{4,5},{5,6},{6,7},{7,8},{8,9},{9,10},{10,1... | collective-permute-start | bytes 73736 | tf_op jit(solution)/shard_map/ppermute | solution.py:10
  16.2 4.0 all-to-all-start.1
  22.9 3.1 all-to-all-done.1
  26.0 7.8 %all_to_all.15 = bf16[4,2,3,4096]{3,1,2,0:T(2,128)(2,1)S(1)} all-to-all(bf16[4,2,3,4096]{3,1,2,0:T(2,128)(2,1)S(1)} %copy.39), channel_id=1, replica_groups=mesh['exp'=4,'tp'=32] {'exp'}, dimensions={0} | all-to-all | bytes 393216 | tf_op jit(solution)/shard_map/all_to_all | solution.py:81
  35.7 64.8 %all-gather.3.cloned.1.call-done = bf16[64,4,2,3,4096]{4,1,3,2,0:T(4,128)(2,1)} async-done(((bf16[2,4,2,3,4096]{4,1,3,2,0:T(4,128)(2,1)}), bf16[64,4,2,3,4096]{4,1,3,2,0:T(4,128)(2,1)}) %all-gather.3.cloned.1.call-update) | async-done | bytes 12582928 | tf_op jit(solution)/shard_map/all_gather | solution.py:85
  100.5 11.2 %fusion.57 = (bf16[32,1,4,2,3,4096]{5,2,4,3,1,0:T(4,128)(2,1)}, bf16[32,1,4,2,3,4096]{5,2,4,3,1,0:T(4,128)(2,1)S(1)}) fusion(bf16[32,2,4,2,3,4096]{5,2,4,3,1,0:T(4,128)(2,1)} %bitcast.69), kind=kLoop, calls=%fused_computation.81 | loop fusion | bytes 25165824 | tf_op jit(solution)/shard_map/slice | solution.py:88
  111.6 5.7 %copy.54 = bf16[32,1,4,2,3,4096]{5,2,0,4,3,1:T(4,128)(2,1)} copy(bf16[32,1,4,2,3,4096]{5,2,4,3,1,0:T(4,128)(2,1)S(1)} %get-tuple-element.8) | data formatting | bytes 12582912
  117.4 9.7 %reshape_squeeze.12 = bf16[128,2,3,4096]{3,0,2,1:T(8,128)(2,1)} reshape(bf16[32,1,4,2,3,4096]{5,2,0,4,3,1:T(4,128)(2,1)} %copy.54) | data formatting | bytes 12582912 | tf_op jit(solution)/shard_map/reshape;squeeze | solution.py:87
  127.1 9.4 %fusion.23 = f32[128,2,3,448]{0,3,2,1:T(8,128)} fusion(bf16[128,2,3,4096]{3,0,2,1:T(8,128)(2,1)} %reshape_squeeze.12, bf16[2,4096,448]{1,2,0:T(8,128)(2,1)} %param.15), kind=kOutput, calls=%fused_computation.21 | convolution fusion | flops 2818572288 | bytes 15007744 | tf_op jit(solution)/shard_map/mjsd,jdf->mjsf/dot_general | solution.py:14
  136.5 7.2 %fusion.26 = f32[128,2,3,448]{0,3,2,1:T(8,128)} fusion(bf16[128,2,3,4096]{3,0,2,1:T(8,128)(2,1)S(1)} %copy-done.1, bf16[2,4096,448]{1,2,0:T(8,128)(2,1)} %param.16), kind=kOutput, calls=%fused_computation.22 | convolution fusion | flops 2818572288 | bytes 15007744 | tf_op jit(solution)/shard_map/mjsd,jdf->mjsf/dot_general | solution.py:17
  143.7 5.7 %copy.55 = bf16[32,1,4,2,3,4096]{5,2,0,4,3,1:T(4,128)(2,1)} copy(bf16[32,1,4,2,3,4096]{5,2,4,3,1,0:T(4,128)(2,1)S(1)} %bitcast.66) | data formatting | bytes 12582912
  149.5 9.9 %reshape_squeeze.13 = bf16[128,2,3,4096]{3,0,2,1:T(8,128)(2,1)} reshape(bf16[32,1,4,2,3,4096]{5,2,0,4,3,1:T(4,128)(2,1)} %copy.55) | data formatting | bytes 12582912 | tf_op jit(solution)/shard_map/reshape;squeeze | solution.py:88
  159.3 8.7 %fusion.20 = f32[128,2,3,448]{0,3,2,1:T(8,128)S(1)} fusion(bf16[128,2,3,4096]{3,0,2,1:T(8,128)(2,1)} %reshape_squeeze.13, bf16[2,448,4096]{2,1,0:T(8,128)(2,1)} %param.17), kind=kOutput, calls=%fused_computation.20 | convolution fusion | flops 2818572288 | bytes 15007744 | tf_op jit(solution)/shard_map/mjsd,jfd->mjsf/dot_general | solution.py:24
  168.0 9.8 %fusion.17 = bf16[128,2,3,4096]{3,0,2,1:T(8,128)(2,1)} fusion(bf16[2,448,4096]{2,1,0:T(8,128)(2,1)} %param.17, f32[128,2,3,448]{0,3,2,1:T(8,128)S(1)} %copy-done.4, f32[128,2,3,448]{0,3,2,1:T(8,128)S(1)} %copy-done.2), kind=kOutput, calls=%fused_computation.17 | convolution fusion | flops 2823782400 | bytes 16384000 | tf_op jit(solution)/shard_map/mjsf,jfd->mjsd/dot_general | solution.py:21
  177.8 6.6 %fusion.3 = f32[2,128,3,4096]{3,1,2,0:T(8,128)} fusion(bf16[2,4096,448]{1,2,0:T(8,128)(2,1)S(1)} %bitcast.71, f32[128,2,3,448]{0,3,2,1:T(8,128)S(1)} %copy-done.2, f32[128,2,3,448]{0,3,2,1:T(8,128)S(1)} %fusion.20, f32[128,2,3,448]{0,3,2,1:T(8,128)S(1)} %copy-done.4), kind=kOutput, calls=%fused_computation.7 | convolution fusion | flops 2822012928 | bytes 24051712 | tf_op jit(solution)/shard_map/mjsf,jdf->mjsd/dot_general | solution.py:31
  184.4 11.1 %fusion.14 = bf16[128,2,3,4096]{3,0,2,1:T(8,128)(2,1)S(1)} fusion(f32[2,128,3,4096]{3,1,2,0:T(8,128)} %fusion.3, bf16[2,4096,448]{1,2,0:T(8,128)(2,1)} %param.16, f32[128,2,3,448]{0,3,2,1:T(8,128)} %copy-done.3, f32[128,2,3,448]{0,3,2,1:T(8,128)} %fusion.23), kind=kOutput, calls=%fused_computation.16 | convolution fusion | flops 2826928128 | bytes 28966912 | tf_op jit(solution)/shard_map/mjsf,jdf->mjsd/dot_general | solution.py:33
  195.6 12.8 %copy.53 = bf16[128,2,3,4096]{3,1,2,0:T(2,128)(2,1)S(1)} copy(bf16[128,2,3,4096]{3,0,2,1:T(8,128)(2,1)S(1)} %fusion.14) | data formatting | bytes 12582912 | tf_op jit(solution)/shard_map/stack;reshape | solution.py:93
  208.4 12.8 %copy.52 = bf16[128,2,3,4096]{3,1,2,0:T(2,128)(2,1)S(1)} copy(bf16[128,2,3,4096]{3,0,2,1:T(8,128)(2,1)S(1)} %copy-done) | data formatting | bytes 12582912 | tf_op jit(solution)/shard_map/stack;reshape | solution.py:93
  221.3 18.0 %pad_maximum_fusion = bf16[32,2,4,2,3,4096]{5,3,4,1,2,0:T(2,128)(2,1)} fusion(bf16[32,1,4,2,3,4096]{5,3,4,1,2,0:T(2,128)(2,1)S(1)} %bitcast.67, bf16[32,1,4,2,3,4096]{5,3,4,1,2,0:T(2,128)(2,1)S(1)} %bitcast.68), kind=kLoop, calls=%fused_computation.2 | loop fusion | flops 6291456 | bytes 25165824 | tf_op jit(solution)/shard_map/stack | solution.py:93
  240.1 132.0 %all-reduce.2.cloned.1.call-done = bf16[32,2,4,2,3,4096]{5,3,4,1,2,0:T(2,128)(2,1)} async-done(((bf16[32,2,4,2,3,4096]{5,3,4,1,2,0:T(2,128)(2,1)}), bf16[32,2,4,2,3,4096]{5,3,4,1,2,0:T(2,128)(2,1)}) %all-reduce.2.cloned.1.call-update) | async-done | bytes 12582928 | tf_op jit(solution)/shard_map/psum | solution.py:100
  372.0 2.2 fusion.31
  374.2 4.0 all-to-all-start.2
  378.2 7.0 %all-to-all-done.2 = bf16[2,4,2,3,4096]{4,2,3,0,1:T(2,128)(2,1)S(1)} async-done(((bf16[2,4,2,3,4096]{4,2,3,0,1:T(2,128)(2,1)}), bf16[2,4,2,3,4096]{4,2,3,0,1:T(2,128)(2,1)S(1)}, u32[]{:S(2)}, u32[]{:S(2)}) %all-to-all-start.2) | async-done | bytes 393248 | tf_op jit(solution)/shard_map/all_to_all | solution.py:102
  389.0 3.9 collective-permute-start.1
  (71 shorter events, 16.2 us)
Async XLA Ops:
  8.0 14.1 %collective-permute-start = (bf16[3,4096]{1,0:T(4,128)(2,1)S(1)}, bf16[3,4096]{1,0:T(4,128)(2,1)S(1)}, u32[]{:S(2)}, u32[]{:S(2)}) collective-permute-start(bf16[3,4096]{1,0:T(4,128)(2,1)S(1)} %slice.55), channel_id=1, source_target_pairs={{0,1},{1,2},{2,3},{3,4},{4,5},{5,6},{6,7},{7,8},{8,9},{9,10},{10,1... | collective-permute-start | bytes 73736 | tf_op jit(solution)/shard_map/ppermute | solution.py:10
  16.2 9.8 %all-to-all-start.1 = ((bf16[4,2,3,4096]{3,1,2,0:T(2,128)(2,1)}), bf16[4,2,3,4096]{3,1,2,0:T(2,128)(2,1)S(1)}, u32[]{:S(2)}, u32[]{:S(2)}) async-start(bf16[4,2,3,4096]{3,1,2,0:T(2,128)(2,1)} %copy.40), calls=%async_computation.1 | async-start | bytes 393216 | tf_op jit(solution)/shard_map/all_to_all | solution.py:82
  20.2 80.3 %all-gather.3.cloned.1.call-start = ((), (), s32[]{:S(2)}) async-start(), calls=%async_computation.4 | async-start | bytes 12976128 | tf_op jit(solution)/shard_map/all_gather | solution.py:85
  35.5 336.6 %all-reduce.2.cloned.1.call-start = ((), (), s32[]{:S(2)}) async-start(), calls=%async_computation.3 | async-start | bytes 25165824 | tf_op jit(solution)/shard_map/psum | solution.py:100
  127.1 9.4 %copy-start.1 = (bf16[128,2,3,4096]{3,0,2,1:T(8,128)(2,1)S(1)}, bf16[128,2,3,4096]{3,0,2,1:T(8,128)(2,1)}, u32[]{:S(2)}) copy-start(bf16[128,2,3,4096]{3,0,2,1:T(8,128)(2,1)} %reshape_squeeze.12) | copy-start | bytes 18874372
  127.1 16.7 %slice-start = ((s8[6291456]{0:T(1024)(128)(4,1)}), s8[4194304]{0:T(1024)(128)(4,1)S(1)}, s32[]{:S(2)}) async-start(s8[6291456]{0:T(1024)(128)(4,1)} %bitcast.65), calls=%async_computation.5 | async-start | bytes 8388608
  136.5 7.2 %slice-start.1 = ((s8[6291456]{0:T(1024)(128)(4,1)}), s8[2097152]{0:T(1024)(128)(4,1)S(1)}, s32[]{:S(2)}) async-start(s8[6291456]{0:T(1024)(128)(4,1)} %bitcast.65), calls=%async_computation.6 | async-start | bytes 4194304
  149.5 28.3 %slice-start.2 = ((s8[7340032]{0:T(1024)(128)(4,1)}), s8[3145728]{0:T(1024)(128)(4,1)S(1)}, s32[]{:S(2)}) async-start(s8[7340032]{0:T(1024)(128)(4,1)} %bitcast.70), calls=%async_computation.7 | async-start | bytes 6291456
  159.3 8.7 %copy-start.2 = (f32[128,2,3,448]{0,3,2,1:T(8,128)S(1)}, f32[128,2,3,448]{0,3,2,1:T(8,128)}, u32[]{:S(2)}) copy-start(f32[128,2,3,448]{0,3,2,1:T(8,128)} %fusion.23) | copy-start | bytes 4128772
  159.3 8.7 %copy-start.4 = (f32[128,2,3,448]{0,3,2,1:T(8,128)S(1)}, f32[128,2,3,448]{0,3,2,1:T(8,128)}, u32[]{:S(2)}) copy-start(f32[128,2,3,448]{0,3,2,1:T(8,128)} %fusion.26) | copy-start | bytes 4128772
  159.3 18.5 %slice-start.3 = ((s8[7340032]{0:T(1024)(128)(4,1)}), s8[4194304]{0:T(1024)(128)(4,1)S(1)}, s32[]{:S(2)}) async-start(s8[7340032]{0:T(1024)(128)(4,1)} %bitcast.70), calls=%async_computation.8 | async-start | bytes 8388608
  168.0 9.8 %copy-start.3 = (f32[128,2,3,448]{0,3,2,1:T(8,128)}, f32[128,2,3,448]{0,3,2,1:T(8,128)S(1)}, u32[]{:S(2)}) copy-start(f32[128,2,3,448]{0,3,2,1:T(8,128)S(1)} %fusion.20) | copy-start | bytes 4128772
  195.6 12.9 %copy-start = (bf16[128,2,3,4096]{3,0,2,1:T(8,128)(2,1)S(1)}, bf16[128,2,3,4096]{3,0,2,1:T(8,128)(2,1)}, u32[]{:S(2)}) copy-start(bf16[128,2,3,4096]{3,0,2,1:T(8,128)(2,1)} %fusion.17) | copy-start | bytes 18874372
  239.3 0.7 copy-start.6
  374.2 11.0 %all-to-all-start.2 = ((bf16[2,4,2,3,4096]{4,2,3,0,1:T(2,128)(2,1)}), bf16[2,4,2,3,4096]{4,2,3,0,1:T(2,128)(2,1)S(1)}, u32[]{:S(2)}, u32[]{:S(2)}) async-start(bf16[2,4,2,3,4096]{4,2,3,0,1:T(2,128)(2,1)} %fusion.31), calls=%async_computation.2 | async-start | bytes 786432 | tf_op jit(solution)/shard_map/all_to_all | solution.py:102
  378.2 10.7 %copy-start.5 = (bf16[8,4096]{1,0:T(8,128)(2,1)S(1)}, bf16[8,4096]{1,0:T(8,128)(2,1)}, u32[]{:S(2)}) copy-start(bf16[8,4096]{1,0:T(8,128)(2,1)} %param.14) | copy-start | bytes 196612
  389.0 5.9 %collective-permute-start.1 = (bf16[3,4096]{1,0:T(4,128)(2,1)S(1)}, bf16[3,4096]{1,0:T(4,128)(2,1)S(1)}, u32[]{:S(2)}, u32[]{:S(2)}) collective-permute-start(bf16[3,4096]{1,0:T(4,128)(2,1)S(1)} %slice.127), channel_id=1, source_target_pairs={{1,0},{2,1},{3,2},{4,3},{5,4},{6,5},{7,6},{8,7},{9,8},{10,9},{11,1... | collective-permute-start | bytes 73736 | tf_op jit(solution)/shard_map/ppermute | solution.py:10
Sparse Core Ops, SparseCore 0:
  35.6 64.8 all-gather.2
  239.5 132.5 all-reduce.1
where the time goes:
time: 405 us; the launch traced here: 403 us
  waiting for transfers between devices  208 us (51%)
  local copies, waits for them, and re-layouts  76.9 us (19%)
  matrix products  54.2 us (13%)
  other arithmetic  24.4 us (6%)
  starting transfers between devices  16.7 us (4%)
  between operations  14.3 us (4%)
  blocking collectives  7.82 us (2%)
    psum x1, waiting for transfers between devices, per_device(): summed = lax.psum(partials, 'tp').astype(jnp.float32)  132 us
    all_gather x1, waiting for transfers between devices, per_device(): piece = lax.all_gather(stacked, 'tp', axis=0, tiled=True)  64.8 us
    another operation x2, local copies, waits for them, and re-layouts, per_device(): jnp.stack([forward_part.astype(jnp.bfloat16).reshape(shape_back), backwar...  25.7 us
    another operation x1, other arithmetic, per_device(): jnp.stack([forward_part.astype(jnp.bfloat16).reshape(shape_back), backwar...  18 us
    unnamed x26, local copies, waits for them, and re-layouts  13 us
    slice x1, local copies, waits for them, and re-layouts, per_device(): piece[:, 1].reshape(piece_rows * groups, per_group, slot_count, model_width)  11.2 us
    dot_general x1, matrix products, expert_rows(): jnp.einsum('mjsf,jdf->mjsd', grad_up, up_weight, preferred_element_type=j...  11.1 us
    another operation x1, local copies, waits for them, and re-layouts, per_device(): piece[:, 1].reshape(piece_rows * groups, per_group, slot_count, model_width)  9.86 us
  transfers between devices with their start and end apart: 6, of which 5 were waited for; matrix products, arithmetic and copies ran while one was open for 2% of the time, Pallas kernels for 0%

commit v1 on v0

v1 whole, which is shorter than its diff:
```python
import jax
import jax.numpy as jnp
import ml_dtypes
import numpy as np
from jax import lax
from jax.experimental import pallas as pl
from jax.experimental.pallas import tpu as pltpu
from jax.sharding import PartitionSpec as P

MESH = pl.DeviceIdType.MESH
BF16, F32 = jnp.bfloat16, jnp.float32
RING = 4
CORES = 2
SLOTS = 3
PEERS = 8
ROWS = PEERS * SLOTS
CHUNKS = 4
NT = (((1,), (1,)), ((), ()))


def moe_kernel(
    mc, disp, sel, ret, gates, gw, uw, dw, out,
    pk, xr, buf, wgu, wd, lhs, acc_gu, acc_b, hid, gg,
    res, rel, ful, part, rel2, ful2, fin, pk2, yr,
    w_local, w_send, w_recv, x_send, x_recv, g_send, g_recv, r_send, r_recv, y_send, y_recv,
):
    width = mc.shape[1]
    dc = width // CHUNKS
    half = dc // 2
    f = gw.shape[1]
    rows = RING * RING * ROWS
    x, t = lax.axis_index("exp"), lax.axis_index("tp")
    z, y, c = t // (RING * CORES), (t // CORES) % RING, t % CORES
    q = x * CORES + c
    sent = []

    def device(x, z, y, c):
        return (x, (z * RING + y) * CORES + c)

    def step_y(by):
        return device(x, z, (y + by) % RING, c)

    def step_z(by):
        return device(x, (z + by) % RING, y, c)

    first, second = (y, z), (z, y)
    step_first, step_second = (step_y, step_z), (step_z, step_y)

    def remote(src, dst, send_sem, recv_sem, to):
        copy = pltpu.make_async_remote_copy(
            src_ref=src, dst_ref=dst, send_sem=send_sem, recv_sem=recv_sem,
            device_id=to, device_id_type=MESH,
        )
        copy.start()
        sent.append(copy)
        return copy

    peers = []
    for dx in range(PEERS // CORES):
        for dcore in range(CORES):
            if dx or dcore:
                px, pc = (x + dx) % (PEERS // CORES), (c + dcore) % CORES
                peers.append((dx * CORES + dcore, px * CORES + pc, device(px, z, y, pc)))
    barrier = pltpu.get_barrier_semaphore()
    partners = [to for _, _, to in peers] + [s(by) for s in step_first for by in (1, -1)]
    for to in partners:
        pl.semaphore_signal(barrier, inc=1, device_id=to, device_id_type=MESH)

    for k in range(CHUNKS):
        cols = pl.ds(k * dc, dc)
        packed = jnp.dot(disp[...], mc[:, cols], preferred_element_type=F32)
        pk[:, :, cols] = packed.reshape(PEERS, 8, dc).astype(BF16)
    pl.semaphore_wait(barrier, len(partners))

    exchanged = {}
    for k in range(CHUNKS):
        cols = pl.ds(k * dc, dc)
        for n, p, to in peers:
            exchanged[k, n] = remote(
                pk.at[p, :, cols], xr.at[q, :, cols], x_send.at[k, n], x_recv.at[k, n], to
            )
    xr[q] = pk[q]

    sibling = device(x, z, y, 1 - c)
    weights, swapped = [], []
    for n, (w, into, at) in enumerate(((gw, wgu, 0), (uw, wgu, 2 * f), (dw, wd, 0))):
        copy = pltpu.make_async_copy(w.at[c], into.at[pl.ds(at, f)], w_local.at[n])
        copy.start()
        weights.append(copy)
        swapped.append(
            remote(w.at[1 - c], into.at[pl.ds(at + f, f)], w_send.at[n], w_recv.at[n], sibling)
        )

    gathering = {}

    def gather_view(a, k, phase, j, h=None):
        if phase == 0:
            v = buf.at[a, k, second[a], j]
            return v if h is None else v.at[:, pl.ds(h * half, half)]
        v = buf.at[a, k, j]
        return v if h is None else v.at[pl.ds(h * 2, 2)]

    def gather_send(k, phase):
        for a in range(2):
            own, to = (first, second)[phase][a], (step_first, step_second)[phase][a]
            v = gather_view(a, k, phase, own)
            for m, by in ((0, 1), (1, -1)):
                gathering[a, k, phase, m] = remote(
                    v, v, g_send.at[a, k, phase, m], g_recv.at[a, k, phase, m], to(by)
                )

    def gather_relay(k, phase):
        for a in range(2):
            own, to = (first, second)[phase][a], (step_first, step_second)[phase][a]
            for m, by in ((0, 1), (1, -1)):
                gathering[a, k, phase, m].wait_recv()
                v = gather_view(a, k, phase, (own - by) % RING, m)
                gathering[a, k, phase, m + 2] = remote(
                    v, v, g_send.at[a, k, phase, m + 2], g_recv.at[a, k, phase, m + 2], to(by)
                )

    def gather_wait(k, phase):
        for a in range(2):
            for m in (2, 3):
                gathering[a, k, phase, m].wait_recv()

    def select(k):
        cols = pl.ds(k * dc, dc)
        for n, _, _ in peers:
            exchanged[k, n].wait_recv()
        got = xr[:, :, cols].astype(F32).reshape(PEERS * 8, dc).astype(BF16)
        own = jnp.dot(sel[...], got, preferred_element_type=F32)
        for a in range(2):
            buf[a, k, second[a], first[a]] = own[a * ROWS : (a + 1) * ROWS].astype(BF16)

    def products(k):
        slab = RING * ROWS
        for s in range(RING):
            for a, v in ((0, buf[0, k, s]), (1, buf[1, k, :, s])):
                lhs[a, s * slab : (s + 1) * slab] = v.astype(F32).reshape(slab, dc).astype(BF16)
        cols = pl.ds(k * dc, dc)

        def add(acc, a, w, at, n):
            made = lax.dot_general(lhs[a], w[pl.ds(at, n), cols], NT, preferred_element_type=F32)
            acc[:, pl.ds(at, n)] = made if k == 0 else acc[:, pl.ds(at, n)] + made

        def tile(i, carry):
            add(acc_gu, 0, wgu, pl.multiple_of(i * 256, 256), 256)
            return carry

        lax.fori_loop(0, 4 * f // 256, tile, 0)

        def tile_b(i, carry):
            add(acc_b, 1, wd, pl.multiple_of(i * 256, 256), 256)
            return carry

        lax.fori_loop(0, 2 * f // 256, tile_b, 0)
        if 2 * f % 256:
            add(acc_b, 1, wd, 2 * f // 256 * 256, 2 * f % 256)

    def activate():
        def strip(i, carry):
            r = pl.ds(pl.multiple_of(i * 16, 16), 16)
            gate_pre, up_pre = acc_gu[r, : 2 * f], acc_gu[r, 2 * f :]
            back = acc_b[r, :]
            s = jax.nn.sigmoid(gate_pre)
            silu = gate_pre * s
            hid[r, :] = (silu * up_pre).astype(BF16)
            gg[r, : 2 * f] = (back * up_pre * s * (1.0 + gate_pre * (1.0 - s))).astype(BF16)
            gg[r, 2 * f :] = (back * silu).astype(BF16)
            return carry

        lax.fori_loop(0, rows // 16, strip, 0)

    def outputs(k):
        def tile(i, carry):
            at = pl.multiple_of(i * 256, 256)
            cols = pl.ds(k * dc + at, 256)
            forward = jnp.dot(hid[...], wd[:, cols], preferred_element_type=F32)
            res[0, k, :, :, :, pl.ds(at, 256)] = forward.reshape(RING, RING, ROWS, 256).astype(BF16)
            backward = jnp.dot(gg[...], wgu[:, cols], preferred_element_type=F32)
            backward = backward.reshape(RING, RING, ROWS, 256).astype(BF16)
            for s in range(RING):
                res[1, k, :, s, :, pl.ds(at, 256)] = backward[s]
            return carry

        lax.fori_loop(0, dc // 256, tile, 0)

    reducing = {}

    def partial(a, k, phase, j, h=None):
        if phase == 0:
            v = res.at[a, k, j]
            return v if h is None else v.at[pl.ds(h * 2, 2)]
        v = part.at[a, k, j]
        return v if h is None else v.at[:, pl.ds(h * half, half)]

    def reduce_relay(k, phase):
        for a in range(2):
            own, to = (second, first)[phase][a], (step_second, step_first)[phase][a]
            for m, by in ((0, 1), (1, -1)):
                reducing[a, k, phase, m] = remote(
                    partial(a, k, phase, (own + 2) % RING, m), (rel, rel2)[phase].at[a, k, m],
                    r_send.at[a, k, phase, m], r_recv.at[a, k, phase, m], to(by),
                )

    def reduce_send(k, phase):
        for a in range(2):
            own, to = (second, first)[phase][a], (step_second, step_first)[phase][a]
            for m, by in ((0, 1), (1, -1)):
                reducing[a, k, phase, m].wait_recv()
                j = (own + by) % RING
                mine, came = partial(a, k, phase, j, m), (rel, rel2)[phase]
                mine[...] = (mine[...].astype(F32) + came[a, k, m].astype(F32)).astype(BF16)
                reducing[a, k, phase, m + 2] = remote(
                    partial(a, k, phase, j), (ful, ful2)[phase].at[a, k, m],
                    r_send.at[a, k, phase, m + 2], r_recv.at[a, k, phase, m + 2], to(by),
                )

    def reduce_sum(k, phase):
        for a in range(2):
            own = (second, first)[phase][a]
            for m in (2, 3):
                reducing[a, k, phase, m].wait_recv()
            came = (ful, ful2)[phase]
            total = partial(a, k, phase, own)[...].astype(F32)
            total = total + came[a, k, 0].astype(F32) + came[a, k, 1].astype(F32)
            if phase == 0:
                part[a, k] = total.astype(BF16)
            else:
                fin[a * ROWS : (a + 1) * ROWS, :] = total

    returned = {}

    def give_back(k):
        cols = pl.ds(k * dc, dc)
        packed = jnp.dot(ret[...], fin[...].astype(BF16), preferred_element_type=F32)
        pk2[:, :, cols] = packed.reshape(PEERS, 8, dc).astype(BF16)
        for n, p, to in peers:
            returned[k, n] = remote(
                pk2.at[p, :, cols], yr.at[q, :, cols], y_send.at[k, n], y_recv.at[k, n], to
            )
        yr[q, :, cols] = pk2[q, :, cols]

    def combine(k):
        cols = pl.ds(k * dc, dc)
        for n, _, _ in peers:
            returned[k, n].wait_recv()
        got = yr[:, :, cols].astype(F32).reshape(PEERS * 8, dc)
        out[:, cols] = jnp.dot(
            gates[...], got, preferred_element_type=F32, precision=lax.Precision.HIGHEST
        )

    def gather_start(k):
        gather_wait(k, 0)
        gather_send(k, 1)

    def gather_end(k):
        gather_wait(k, 1)
        products(k)

    def reduce_next(k):
        reduce_sum(k, 0)
        reduce_relay(k, 1)

    def reduce_end(k):
        reduce_sum(k, 1)
        give_back(k)

    for k in range(CHUNKS):
        select(k)
        gather_send(k, 0)
        if k >= 1:
            gather_relay(k - 1, 0)
        if k >= 2:
            gather_start(k - 2)
    gather_relay(CHUNKS - 1, 0)
    for k in range(CHUNKS):
        gather_relay(k, 1)
        if k + 2 < CHUNKS:
            gather_start(k + 2)
        if k == 0:
            for copy in weights:
                copy.wait()
            for copy in swapped:
                copy.wait_recv()
        else:
            gather_end(k - 1)
    gather_end(CHUNKS - 1)
    activate()
    for s in range(CHUNKS + 4):
        if s < CHUNKS:
            outputs(s)
            reduce_relay(s, 0)
        if 0 <= s - 1 < CHUNKS:
            reduce_send(s - 1, 0)
        if 0 <= s - 2 < CHUNKS:
            reduce_next(s - 2)
        if 0 <= s - 3 < CHUNKS:
            reduce_send(s - 3, 1)
        if 0 <= s - 4 < CHUNKS:
            reduce_end(s - 4)
    for k in range(CHUNKS):
        combine(k)
    for copy in sent:
        copy.wait_send()


def moe(mc, disp, sel, ret, gates, gw, uw, dw):
    width, f = mc.shape[1], gw.shape[1]
    dc = width // CHUNKS
    rows = RING * RING * ROWS
    vmem = pl.BlockSpec(memory_space=pltpu.VMEM)
    hbm = pl.BlockSpec(memory_space=pl.ANY)
    dma = pltpu.SemaphoreType.DMA
    flops = 6 * 2 * rows * width * 2 * f
    return pl.pallas_call(
        moe_kernel,
        out_shape=jax.ShapeDtypeStruct((16, width), F32),
        in_specs=[vmem] * 5 + [hbm] * 3,
        out_specs=vmem,
        scratch_shapes=[
            pltpu.VMEM((PEERS, 8, width), BF16),
            pltpu.VMEM((PEERS, 8, width), BF16),
            pltpu.VMEM((2, CHUNKS, RING, RING, ROWS, dc), BF16),
            pltpu.VMEM((4 * f, width), BF16),
            pltpu.VMEM((2 * f, width), BF16),
            pltpu.VMEM((2, rows, dc), BF16),
            pltpu.VMEM((rows, 4 * f), F32),
            pltpu.VMEM((rows, 2 * f), F32),
            pltpu.VMEM((rows, 2 * f), BF16),
            pltpu.VMEM((rows, 4 * f), BF16),
            pltpu.VMEM((2, CHUNKS, RING, RING, ROWS, dc), BF16),
            pltpu.VMEM((2, CHUNKS, 2, 2, ROWS, dc), BF16),
            pltpu.VMEM((2, CHUNKS, 2, RING, ROWS, dc), BF16),
            pltpu.VMEM((2, CHUNKS, RING, ROWS, dc), BF16),
            pltpu.VMEM((2, CHUNKS, 2, ROWS, dc // 2), BF16),
            pltpu.VMEM((2, CHUNKS, 2, ROWS, dc), BF16),
            pltpu.VMEM((2 * ROWS, dc), F32),
            pltpu.VMEM((PEERS, 8, width), BF16),
            pltpu.VMEM((PEERS, 8, width), BF16),
            dma((3,)),
            dma((3,)),
            dma((3,)),
            dma((CHUNKS, PEERS)),
            dma((CHUNKS, PEERS)),
            dma((2, CHUNKS, 2, 4)),
            dma((2, CHUNKS, 2, 4)),
            dma((2, CHUNKS, 2, 4)),
            dma((2, CHUNKS, 2, 4)),
            dma((CHUNKS, PEERS)),
            dma((CHUNKS, PEERS)),
        ],
        compiler_params=pltpu.CompilerParams(
            collective_id=0, has_side_effects=True, vmem_limit_bytes=58 << 20
        ),
        cost_estimate=pl.CostEstimate(
            flops=flops, bytes_accessed=12 * f * width, transcendentals=rows * 2 * f
        ),
    )(mc, disp, sel, ret, gates, gw, uw, dw)


def shifted(array, axis, by):
    size = lax.axis_size(axis)
    pairs = [(i, i + by) for i in range(size) if 0 <= i + by < size]
    return lax.ppermute(array, axis, pairs)


def row_maps():
    sel = np.zeros((2 * ROWS, PEERS * 8), ml_dtypes.bfloat16)
    for a in range(2):
        for s in range(PEERS):
            for n in range(SLOTS):
                sel[a * ROWS + s * SLOTS + n, s * 8 + a * SLOTS + n] = 1
    return jnp.asarray(sel), jnp.asarray(sel.T.copy())


def per_device(
    inputs, conv_weight, expert_ids, gate_values, cotangent, gate_weight, up_weight, down_weight
):
    tok_rows = inputs.shape[0]
    kernel = conv_weight.shape[0]
    source = inputs.astype(F32)
    rim_rows = shifted(inputs[tok_rows - (kernel - 1) :], ("exp", "tp"), 1)
    extended = jnp.concatenate([rim_rows.astype(F32), source], 0)
    conv_sum = source
    for j in range(kernel):
        conv_sum = conv_sum + conv_weight[j] * extended[kernel - 1 - j : kernel - 1 - j + tok_rows]
    mixed = conv_sum.astype(BF16)

    flat_ids = expert_ids.reshape(-1)
    order = jnp.arange(flat_ids.shape[0])
    same = (flat_ids[:, None] == flat_ids[None, :]) & (order[None, :] < order[:, None])
    slot = jnp.sum(same.astype(jnp.int32), 1).reshape(expert_ids.shape)
    target = expert_ids * 8 + slot
    places = jnp.arange(PEERS * 8, dtype=jnp.int32)
    hit_in = places[None, None, :] == target[:, :, None]
    hit_grad = places[None, None, :] == target[:, :, None] + SLOTS
    disp = jnp.concatenate([jnp.any(hit_in, 1), jnp.any(hit_grad, 1)], 0).astype(BF16).T
    gates = jnp.concatenate(
        [jnp.sum(jnp.where(hit, gate_values[:, :, None], 0.0), 1) for hit in (hit_in, hit_grad)], 0
    )
    sel, ret = row_maps()
    moe_sums = moe(
        jnp.concatenate([mixed, cotangent], 0), disp, sel, ret, gates,
        jnp.swapaxes(gate_weight, 1, 2), jnp.swapaxes(up_weight, 1, 2), down_weight,
    )
    result = (mixed.astype(F32) + moe_sums[:tok_rows]).astype(BF16)
    grad_mixed = cotangent.astype(F32) + moe_sums[tok_rows:]
    next_rows = shifted(grad_mixed[: kernel - 1].astype(BF16), ("exp", "tp"), -1).astype(F32)
    extended_grad = jnp.concatenate([grad_mixed, next_rows], 0)
    grad_sum = grad_mixed
    for j in range(kernel):
        grad_sum = grad_sum + conv_weight[j] * extended_grad[j : j + tok_rows]
    return (result, grad_sum.astype(BF16))


def solution(mesh):
    in_specs = (
        P(("exp", "tp"), None),
        P(),
        P(("exp", "tp"), None),
        P(("exp", "tp"), None),
        P(("exp", "tp"), None),
        P("exp", None, "tp"),
        P("exp", None, "tp"),
        P("exp", "tp", None),
    )
    out_specs = (P(("exp", "tp"), None), P(("exp", "tp"), None))
    return jax.shard_map(
        per_device, mesh=mesh, in_specs=in_specs, out_specs=out_specs, check_vma=False
    )
```

time: 405 us -> 127 us (0.31)
  waiting for transfers between devices: 208 us -> 3.03 us
  Pallas kernels: 0 us -> 105 us
  local copies, waits for them, and re-layouts: 76.9 us -> 3.71 us
  matrix products: 54.2 us -> 0 us
  other arithmetic: 24.4 us -> 6.49 us
  between operations: 14.3 us -> 0.69 us
  starting transfers between devices: 16.7 us -> 6.93 us
  blocking collectives: 7.82 us -> 0 us
    psum x1 -> x0, waiting for transfers between devices: 132 us -> none  [per_device(): summed = lax.psum(partials, 'tp').astype(jnp.float32)]
    pallas_call x0 -> x1, Pallas kernels: none -> 105 us  [moe(): pl.pallas_call(moe_kernel, out_shape=jax.ShapeDtypeStruct((16, width), F3...]
    all_gather x1 -> x0, waiting for transfers between devices: 64.8 us -> none  [per_device(): piece = lax.all_gather(stacked, 'tp', axis=0, tiled=True)]
    dot_general x8 -> x0, matrix products: 54.2 us -> none  [the longest x1 11.1 us: expert_rows(): jnp.einsum('mjsf,jdf->mjsd', grad_up, up_weight, preferred_element_type=j...]
    another operation x7 -> x0, local copies, waits for them, and re-layouts: 46.7 us -> none  [the longest x2 25.7 us: per_device(): jnp.stack([forward_part.astype(jnp.bfloat16).reshape(shape_back), backwar...]
    another operation x3 -> x0, other arithmetic: 18.6 us -> none  [the longest x1 18 us: per_device(): jnp.stack([forward_part.astype(jnp.bfloat16).reshape(shape_back), backwar...]
    unnamed x26 -> x3, local copies, waits for them, and re-layouts: 13 us -> 0.76 us
    slice x6 -> x2, local copies, waits for them, and re-layouts: 13.1 us -> 1.07 us  [the longest x1 1.06 us: per_device(): conv_weight[j] * extended[kernel - 1 - j:kernel - 1 - j + tok_rows]]
  transfers between devices with their start and end apart: 6 -> 2, of which waited for: 5 -> 1; matrix products, arithmetic and copies ran while one was open for 2% -> 4% of each run, Pallas kernels for 0% -> 0%
where the time goes in v1:
time: 127 us; the launch traced here: 126 us
  Pallas kernels  105 us (83%)
  starting transfers between devices  6.93 us (5%)
  other arithmetic  6.49 us (5%)
  local copies, waits for them, and re-layouts  3.71 us (3%)
  waiting for transfers between devices  3.03 us (2%)
    pallas_call x1, Pallas kernels, moe(): pl.pallas_call(moe_kernel, out_shape=jax.ShapeDtypeStruct((16, width), F3...  105 us
    ppermute x2, starting transfers between devices, shifted(): return lax.ppermute(array, axis, pairs)  6.93 us
    ppermute x2, waiting for transfers between devices, shifted(): return lax.ppermute(array, axis, pairs)  3.03 us
  transfers between devices with their start and end apart: 2, of which 1 were waited for; matrix products, arithmetic and copies ran while one was open for 4% of the time, Pallas kernels for 0%

profile of v1, /device:TPU:1, one launch (start us, length us, event | category | flops | bytes accessed | tf_op | source)
XLA Modules:
  0.0 125.7 jit_solution(2454763943928823965)
XLA Ops:
  0.6 0.9 slice.49
  1.5 4.6 %collective-permute-start = (bf16[3,4096]{1,0:T(4,128)(2,1)S(1)}, bf16[3,4096]{1,0:T(4,128)(2,1)S(1)}, u32[]{:S(2)}, u32[]{:S(2)}) collective-permute-start(bf16[3,4096]{1,0:T(4,128)(2,1)S(1)} %slice.49), channel_id=1, source_target_pairs={{0,1},{1,2},{2,3},{3,4},{4,5},{5,6},{6,7},{7,8},{8,9},{9,10},{10,1... | collective-permute-start | bytes 73736 | tf_op jit(solution)/shard_map/ppermute | solution.py:366
  6.1 0.8 copy.27
  6.9 0.1 eq.42
  6.9 0.2 convert_reduce_fusion
  7.1 0.1 reshape.13
  7.2 0.1 copy.30
  7.3 0.1 copy.29
  7.4 0.1 fusion.18
  7.5 0.8 select_reduce_fusion.1
  8.2 1.1 fusion.21
  9.3 0.6 pad_maximum_fusion.3.gates
  9.9 0.8 convert_element_type.29
  10.7 0.7 copy.31
  11.4 0.0 collective-permute-done
  11.5 0.1 fusion.3
  11.6 1.5 %pad_maximum_fusion.2.mc = bf16[16,4096]{1,0:T(8,128)(2,1)} fusion(bf16[8,4096]{1,0:T(8,128)(2,1)} %param.14, bf16[8,4096]{1,0:T(8,128)(2,1)S(1)} %fusion.3), kind=kLoop, calls=%fused_computation.30 | loop fusion | flops 262144 | bytes 262144 | tf_op jit(solution)/shard_map/concatenate | solution.py:405
  13.1 0.0 copy-start
  13.1 104.8 %shard_map.113 = f32[16,4096]{1,0:T(8,128)} custom-call(bf16[16,4096]{1,0:T(8,128)(2,1)} %pad_maximum_fusion.2.mc, bf16[64,16]{1,0:T(8,128)(2,1)} %bitcast.15, bf16[48,64]{1,0:T(8,128)(2,1)} %constant.14.clone.sel, bf16[64,48]{1,0:T(8,128)(2,1)} %constant.15.clone.ret, f32[16,64]{1,0:T(8,128)} %pad_maximum_fusion.3.gates, bf16[2,448,4096]{2,1,0:T(8,128)(2,1)} %bitcast.16, ...), custom_call_target="tpu_custom_call" | custom-call | flops 16911433728 | bytes 22020096 | tf_op jit(solution)/shard_map/pallas_call | solution.py:317
  117.9 0.0 copy-done
  117.9 1.6 %slice_add_fusion = (f32[8,4096]{1,0:T(8,128)S(1)}, bf16[8,4096]{1,0:T(8,128)(2,1)}) fusion(f32[16,4096]{1,0:T(8,128)} %shard_map.113, bf16[8,4096]{1,0:T(8,128)(2,1)S(1)} %copy-done, bf16[8,4096]{1,0:T(8,128)(2,1)S(1)} %fusion.3), kind=kLoop, calls=%fused_computation.31 | loop fusion | flops 163840 | bytes 589824 | tf_op jit(solution)/shard_map/add | solution.py:409
  119.6 2.3 %collective-permute-start.1 = (bf16[3,4096]{1,0:T(4,128)(2,1)S(1)}, bf16[3,4096]{1,0:T(4,128)(2,1)S(1)}, u32[]{:S(2)}, u32[]{:S(2)}) collective-permute-start(bf16[3,4096]{1,0:T(4,128)(2,1)S(1)} %slice.113), channel_id=1, source_target_pairs={{1,0},{2,1},{3,2},{4,3},{5,4},{6,5},{7,6},{8,7},{9,8},{10,9},{11,1... | collective-permute-start | bytes 73736 | tf_op jit(solution)/shard_map/ppermute | solution.py:366
  121.9 3.0 %collective-permute-done.1 = bf16[3,4096]{1,0:T(4,128)(2,1)S(1)} collective-permute-done((bf16[3,4096]{1,0:T(4,128)(2,1)S(1)}, bf16[3,4096]{1,0:T(4,128)(2,1)S(1)}, u32[]{:S(2)}, u32[]{:S(2)}) %collective-permute-start.1) | collective-permute-done | bytes 24608 | tf_op jit(solution)/shard_map/ppermute | solution.py:366
  124.9 0.7 fusion.7
  (5 shorter events, 0.0 us)
Async XLA Ops:
  1.5 9.9 %collective-permute-start = (bf16[3,4096]{1,0:T(4,128)(2,1)S(1)}, bf16[3,4096]{1,0:T(4,128)(2,1)S(1)}, u32[]{:S(2)}, u32[]{:S(2)}) collective-permute-start(bf16[3,4096]{1,0:T(4,128)(2,1)S(1)} %slice.49), channel_id=1, source_target_pairs={{0,1},{1,2},{2,3},{3,4},{4,5},{5,6},{6,7},{7,8},{8,9},{9,10},{10,1... | collective-permute-start | bytes 73736 | tf_op jit(solution)/shard_map/ppermute | solution.py:366
  13.1 104.8 %copy-start = (bf16[8,4096]{1,0:T(8,128)(2,1)S(1)}, bf16[8,4096]{1,0:T(8,128)(2,1)}, u32[]{:S(2)}) copy-start(bf16[8,4096]{1,0:T(8,128)(2,1)} %param.14) | copy-start | bytes 196612
  119.6 5.4 %collective-permute-start.1 = (bf16[3,4096]{1,0:T(4,128)(2,1)S(1)}, bf16[3,4096]{1,0:T(4,128)(2,1)S(1)}, u32[]{:S(2)}, u32[]{:S(2)}) collective-permute-start(bf16[3,4096]{1,0:T(4,128)(2,1)S(1)} %slice.113), channel_id=1, source_target_pairs={{1,0},{2,1},{3,2},{4,3},{5,4},{6,5},{7,6},{8,7},{9,8},{10,9},{11,1... | collective-permute-start | bytes 73736 | tf_op jit(solution)/shard_map/ppermute | solution.py:366

commit v2 on v0

v2 whole, which is shorter than its diff:
```python
import jax
import jax.numpy as jnp
import ml_dtypes
import numpy as np
from jax import lax
from jax.experimental import pallas as pl
from jax.experimental.pallas import tpu as pltpu
from jax.sharding import PartitionSpec as P

MESH = pl.DeviceIdType.MESH
BF16, F32 = jnp.bfloat16, jnp.float32
RING = 4
PLANE = RING * RING
CORES = 2
SLOTS = 3
PEERS = 8
BLOCK = 4
TAPS = 4
GROUPS = ((2, 4), (1, 2))
UNITS = [(g, k) for g, (_, pieces) in enumerate(GROUPS) for k in range(pieces)]
NT = (((1,), (1,)), ((), ()))


def moe_kernel(
    inputs, conv, ids, gate_values, cot, sel, ret, gw, uw, dw, result, grad,
    ext, halo_out, halo_in, back_out, back_in, mixed, gates, pk, xr, pk2, yr, wgu, wd, *rest,
):
    per_group, sems = rest[: 13 * len(GROUPS)], rest[13 * len(GROUPS) :]
    buf, lhs, acc_gu, acc_b, hid, gg, res, rel, ful, part, rel2, ful2, fin = (
        per_group[i * len(GROUPS) : (i + 1) * len(GROUPS)] for i in range(13)
    )
    w_sem, h_sem, b_sem, x_send, x_recv, g_send, g_recv, r_send, r_recv, y_send, y_recv = sems
    width = inputs.shape[1]
    f = gw.shape[1]

    x, t = lax.axis_index("exp"), lax.axis_index("tp")
    n_exp, n_tp = PEERS // CORES, PLANE * CORES
    z, y, c = t // (RING * CORES), (t // CORES) % RING, t % CORES
    q = x * CORES + c
    here, devices = x * n_tp + t, n_exp * n_tp

    def rows_of(g):
        return PEERS * GROUPS[g][0]

    def cols_of(u):
        g, k = UNITS[u]
        dc = width // GROUPS[g][1]
        return pl.ds(k * dc, dc)

    def device(x, z, y, c):
        return (x, (z * RING + y) * CORES + c)

    def step_y(by):
        return device(x, z, (y + by) % RING, c)

    def step_z(by):
        return device(x, (z + by) % RING, y, c)

    def line(by):
        v = (here + by) % devices
        return (v // n_tp, v % n_tp)

    axes = ((y, z), (z, y))
    steps = ((step_y, step_z), (step_z, step_y))
    place = [axes[a][1] * RING + axes[a][0] for a in range(2)]

    def remote(src, dst, send_sem, recv_sem, to):
        pltpu.make_async_remote_copy(
            src_ref=src, dst_ref=dst, send_sem=send_sem, recv_sem=recv_sem,
            device_id=to, device_id_type=MESH,
        ).start()

    def wait(sem, like):
        pltpu.make_async_copy(like, like, sem).wait()

    peers = []
    for dx in range(n_exp):
        for dcore in range(CORES):
            if dx or dcore:
                px, pc = (x + dx) % n_exp, (c + dcore) % CORES
                peers.append((px * CORES + pc, device(px, z, y, pc)))
    barrier = pltpu.get_barrier_semaphore()
    partners = [to for _, to in peers] + [s(by) for s in steps[0] for by in (1, -1)]
    partners += [line(1), line(-1)]
    for to in partners:
        pl.semaphore_signal(barrier, inc=1, device_id=to, device_id_type=MESH)

    own = inputs[...].astype(F32)
    ext[8:16, :] = own
    halo_out[...] = own[4:8].astype(BF16)

    r = lax.broadcasted_iota(jnp.int32, (PEERS * 8, 8), 0)
    expert, row = r >> 3, r & 7
    before = lax.broadcasted_iota(jnp.int32, (8, 8), 0) < lax.broadcasted_iota(jnp.int32, (8, 8), 1)
    named = [(expert == ids[k : k + 1, :]).astype(F32) for k in range(2)]
    earlier = jnp.dot(named[0] + named[1], before.astype(F32), preferred_element_type=F32)
    at = [
        jnp.where(row == 4, 2, jnp.where(row < 2, row, -1)),
        jnp.where(row == 5, 2, jnp.where((row == 2) | (row == 3), row - 2, -1)),
    ]
    hit = [(earlier == at[a].astype(F32)).astype(F32) for a in range(2)]
    disp = [((named[0] + named[1]) * hit[a]).astype(BF16) for a in range(2)]
    gate = named[0] * gate_values[0:1, :] + named[1] * gate_values[1:2, :]
    same = lax.broadcasted_iota(jnp.int32, (8, 8), 0) == lax.broadcasted_iota(jnp.int32, (8, 8), 1)
    for a in range(2):
        gates[a * 8 : (a + 1) * 8, :] = lax.dot_general(
            same.astype(F32), gate * hit[a], NT,
            preferred_element_type=F32, precision=lax.Precision.HIGHEST,
        )

    pl.semaphore_wait(barrier, len(partners))
    remote(halo_out, halo_in, h_sem.at[0], h_sem.at[1], line(1))
    wait(h_sem.at[1], halo_in)
    ext[4:8, :] = jnp.where(here == 0, 0.0, halo_in[...].astype(F32))
    total = own
    for j in range(TAPS):
        total = total + conv[j : j + 1, :] * ext[8 - j : 16 - j, :]
    mixed[...] = total.astype(BF16)
    packed = jnp.dot(disp[0], mixed[...], preferred_element_type=F32)
    packed = packed + jnp.dot(disp[1], cot[...], preferred_element_type=F32)
    packed = packed.reshape(PEERS, 8, width)
    pk[0] = packed[:, :BLOCK].astype(BF16)
    pk[1] = packed[:, BLOCK:].astype(BF16)

    for u, (g, _) in enumerate(UNITS):
        cols = cols_of(u)
        for p, to in peers:
            remote(pk.at[g, p, :, cols], xr.at[g, q, :, cols], x_send.at[u], x_recv.at[u], to)
    for g in range(len(GROUPS)):
        xr[g, q] = pk[g, q]

    sibling = device(x, z, y, 1 - c)
    for w, into, first in ((gw, wgu, 0), (uw, wgu, 2 * f), (dw, wd, 0)):
        pltpu.make_async_copy(w.at[c], into.at[pl.ds(first, f)], w_sem.at[0]).start()
        remote(
            w.at[1 - c], into.at[pl.ds(first + f, f)], w_sem.at[1], w_sem.at[2], sibling
        )

    def gather_view(a, u, phase, j, h=None):
        g, k = UNITS[u]
        if phase == 0:
            v = buf[g].at[a, k, axes[a][1] * RING + j]
            half = width // GROUPS[g][1] // 2
            return v if h is None else v.at[:, pl.ds(h * half, half)]
        return buf[g].at[a, k, pl.ds(j * RING, RING) if h is None else pl.ds(j * RING + 2 * h, 2)]

    def blocks(u, n):
        g, k = UNITS[u]
        return buf[g].at[0, k, pl.ds(0, n)]

    def gather_send(u, phase):
        for a in range(2):
            v = gather_view(a, u, phase, axes[a][phase])
            for by in (1, -1):
                remote(v, v, g_send.at[u], g_recv.at[u, phase, 0], steps[a][phase](by))

    def gather_relay(u, phase):
        wait(g_recv.at[u, phase, 0], blocks(u, (4, 16)[phase]))
        for a in range(2):
            for h, by in ((0, 1), (1, -1)):
                v = gather_view(a, u, phase, (axes[a][phase] - by) % RING, h)
                remote(v, v, g_send.at[u], g_recv.at[u, phase, 1], steps[a][phase](by))

    def gather_wait(u, phase):
        wait(g_recv.at[u, phase, 1], blocks(u, (2, 8)[phase]))

    def select(u):
        g, k = UNITS[u]
        cols, n = cols_of(u), rows_of(g)
        wait(x_recv.at[u], xr.at[g, pl.ds(0, PEERS - 1), :, cols])
        got = xr[g, :, :, cols].astype(F32)
        got = jnp.concatenate([got, jnp.zeros_like(got)], 1)
        got = got.reshape(PEERS * 8, got.shape[-1]).astype(BF16)
        first = sum(2 * rows_of(i) for i in range(g))
        mine = jnp.dot(sel[first : first + 2 * n, :], got, preferred_element_type=F32)
        for a in range(2):
            buf[g][a, k, place[a]] = mine[a * n : (a + 1) * n].astype(BF16)

    def products(u):
        g, k = UNITS[u]
        n, cols = rows_of(g), cols_of(u)
        dc, slab = width // GROUPS[g][1], RING * rows_of(g)
        for s in range(RING):
            v = buf[g][0, k, s * RING : (s + 1) * RING].astype(F32)
            lhs[g][0, s * slab : (s + 1) * slab] = v.reshape(slab, dc).astype(BF16)
            v = jnp.stack([buf[g][1, k, j * RING + s] for j in range(RING)], 0).astype(F32)
            lhs[g][1, s * slab : (s + 1) * slab] = v.reshape(slab, dc).astype(BF16)

        def add(acc, a, w, at, n):
            made = lax.dot_general(
                lhs[g][a], w[pl.ds(at, n), cols], NT, preferred_element_type=F32
            )
            acc[:, pl.ds(at, n)] = made if k == 0 else acc[:, pl.ds(at, n)] + made

        def tile(i, carry):
            add(acc_gu[g], 0, wgu, pl.multiple_of(i * 256, 256), 256)
            return carry

        lax.fori_loop(0, 4 * f // 256, tile, 0)

        def tile_b(i, carry):
            add(acc_b[g], 1, wd, pl.multiple_of(i * 256, 256), 256)
            return carry

        lax.fori_loop(0, 2 * f // 256, tile_b, 0)
        if 2 * f % 256:
            add(acc_b[g], 1, wd, 2 * f // 256 * 256, 2 * f % 256)

    def activate(g):
        def strip(i, carry):
            r = pl.ds(pl.multiple_of(i * 16, 16), 16)
            gate_pre, up_pre = acc_gu[g][r, : 2 * f], acc_gu[g][r, 2 * f :]
            back = acc_b[g][r, :]
            s = jax.nn.sigmoid(gate_pre)
            silu = gate_pre * s
            hid[g][r, :] = (silu * up_pre).astype(BF16)
            gg[g][r, : 2 * f] = (back * up_pre * s * (1.0 + gate_pre * (1.0 - s))).astype(BF16)
            gg[g][r, 2 * f :] = (back * silu).astype(BF16)
            return carry

        lax.fori_loop(0, PLANE * rows_of(g) // 16, strip, 0)

    def outputs(u):
        g, k = UNITS[u]
        n, dc = rows_of(g), width // GROUPS[g][1]

        def tile(i, carry):
            at = pl.multiple_of(i * 256, 256)
            cols, to = pl.ds(k * dc + at, 256), pl.ds(at, 256)
            forward = jnp.dot(hid[g][...], wd[:, cols], preferred_element_type=F32)
            res[g][0, k, :, :, to] = forward.reshape(PLANE, n, 256).astype(BF16)
            backward = jnp.dot(gg[g][...], wgu[:, cols], preferred_element_type=F32)
            backward = backward.reshape(RING, RING, n, 256).astype(BF16)
            for s in range(RING):
                res[g][1, k, s * RING : (s + 1) * RING, :, to] = backward[:, s]
            return carry

        lax.fori_loop(0, dc // 256, tile, 0)

    def partial(a, u, phase, j, h=None):
        g, k = UNITS[u]
        if phase == 0:
            return res[g].at[
                a, k, pl.ds(j * RING, RING) if h is None else pl.ds(j * RING + 2 * h, 2)
            ]
        v = part[g].at[a, k, j]
        half = width // GROUPS[g][1] // 2
        return v if h is None else v.at[:, pl.ds(h * half, half)]

    def reduce_relay(u, phase):
        g, k = UNITS[u]
        for a in range(2):
            own, to = axes[a][1 - phase], steps[a][1 - phase]
            for h, by in ((0, 1), (1, -1)):
                remote(
                    partial(a, u, phase, (own + 2) % RING, h), (rel, rel2)[phase][g].at[a, k, h],
                    r_send.at[u], r_recv.at[u, phase, 0], to(by),
                )

    def reduce_send(u, phase):
        g, k = UNITS[u]
        wait(r_recv.at[u, phase, 0], blocks(u, (8, 2)[phase]))
        for a in range(2):
            own, to = axes[a][1 - phase], steps[a][1 - phase]
            for h, by in ((0, 1), (1, -1)):
                j = (own + by) % RING
                mine, came = partial(a, u, phase, j, h), (rel, rel2)[phase][g]
                mine[...] = (mine[...].astype(F32) + came[a, k, h].astype(F32)).astype(BF16)
                remote(
                    partial(a, u, phase, j), (ful, ful2)[phase][g].at[a, k, h],
                    r_send.at[u], r_recv.at[u, phase, 1], to(by),
                )

    def reduce_sum(u, phase):
        g, k = UNITS[u]
        n = rows_of(g)
        wait(r_recv.at[u, phase, 1], blocks(u, (16, 4)[phase]))
        for a in range(2):
            came = (ful, ful2)[phase][g]
            total = partial(a, u, phase, axes[a][1 - phase])[...].astype(F32)
            total = total + came[a, k, 0].astype(F32) + came[a, k, 1].astype(F32)
            if phase == 0:
                part[g][a, k] = total.astype(BF16)
            else:
                fin[g][a * n : (a + 1) * n, :] = total

    def give_back(u):
        g, _ = UNITS[u]
        cols, n = cols_of(u), 2 * rows_of(g)
        back = ret[g * PEERS * 8 : (g + 1) * PEERS * 8, :n]
        packed = jnp.dot(back, fin[g][...].astype(BF16), preferred_element_type=F32)
        packed = packed.reshape(PEERS, 8, packed.shape[-1])[:, :BLOCK].astype(BF16)
        pk2[g, :, :, cols] = packed
        for p, to in peers:
            remote(pk2.at[g, p, :, cols], yr.at[g, q, :, cols], y_send.at[u], y_recv.at[u], to)
        yr[g, q, :, cols] = pk2[g, q, :, cols]

    parts = min(pieces for _, pieces in GROUPS)
    span = width // parts

    def combine(i):
        cols = pl.ds(i * span, span)
        for u, (g, k) in enumerate(UNITS):
            if k * parts // GROUPS[g][1] == i:
                wait(y_recv.at[u], yr.at[g, pl.ds(0, PEERS - 1), :, cols_of(u)])
        got = [yr[g, :, :, cols].astype(F32) for g in range(len(GROUPS))]
        got = jnp.concatenate(got, 1).reshape(PEERS * 8, span)
        sums = jnp.dot(
            gates[...], got, preferred_element_type=F32, precision=lax.Precision.HIGHEST
        )
        result[:, cols] = (mixed[:, cols].astype(F32) + sums[:8]).astype(BF16)
        grad_mixed = cot[:, cols].astype(F32) + sums[8:]
        ext[0:8, cols] = grad_mixed
        back_out[:, cols] = grad_mixed[:4].astype(BF16)
        remote(
            back_out.at[:, cols], back_in.at[:, cols], b_sem.at[0, i], b_sem.at[1, i], line(-1)
        )

    def finish(i):
        cols = pl.ds(i * span, span)
        wait(b_sem.at[1, i], back_in.at[:, cols])
        ext[8:12, cols] = jnp.where(here == devices - 1, 0.0, back_in[:, cols].astype(F32))
        total = ext[0:8, cols]
        for j in range(TAPS):
            total = total + conv[j : j + 1, cols] * ext[j : j + 8, cols]
        grad[:, cols] = total.astype(BF16)

    n = len(UNITS)
    last = GROUPS[0][1] - 1

    def gather_step(s):
        if s < n:
            select(s)
            gather_send(s, 0)
        if 0 <= s - 1 < n:
            gather_relay(s - 1, 0)
        if 0 <= s - 4 < n:
            gather_relay(s - 4, 1)
        if 0 <= s - 2 < n:
            gather_wait(s - 2, 0)
            gather_send(s - 2, 1)

    def gather_end(u):
        if u == 0:
            wait(w_sem.at[0], wgu.at[pl.ds(0, 3 * f)])
            wait(w_sem.at[2], wgu.at[pl.ds(0, 3 * f)])
        gather_wait(u, 1)
        products(u)
        g, k = UNITS[u]
        if k + 1 == GROUPS[g][1]:
            activate(g)

    def reduce_step(s):
        if s < n:
            outputs(s)
            reduce_relay(s, 0)
        if 0 <= s - 1 < n:
            reduce_send(s - 1, 0)
        if 0 <= s - 2 < n:
            reduce_sum(s - 2, 0)
            reduce_relay(s - 2, 1)
        if 0 <= s - 3 < n:
            reduce_send(s - 3, 1)
        if 0 <= s - 4 < n:
            reduce_sum(s - 4, 1)
            give_back(s - 4)

    for s in range(last + 6):
        gather_step(s)
        if s >= 5:
            gather_end(s - 5)
    for s in range(n + 4):
        reduce_step(s)
        if last + 6 + s < n + 5:
            gather_step(last + 6 + s)
            gather_end(last + 1 + s)
    for i in range(parts):
        combine(i)
    for i in range(parts):
        finish(i)

    wait(h_sem.at[0], halo_out)
    wait(w_sem.at[1], wgu.at[pl.ds(0, 3 * f)])
    for i in range(parts):
        wait(b_sem.at[0, i], back_out.at[:, pl.ds(i * span, span)])
    for u, (g, k) in enumerate(UNITS):
        wait(x_send.at[u], xr.at[g, pl.ds(0, PEERS - 1), :, cols_of(u)])
        wait(y_send.at[u], yr.at[g, pl.ds(0, PEERS - 1), :, cols_of(u)])
        wait(g_send.at[u], buf[g].at[:, k, pl.ds(0, PLANE - 1)])
        wait(r_send.at[u], res[g].at[:, k, pl.ds(0, PLANE - 1)])


def moe(inputs, conv, ids, gate_values, cot, sel, ret, gw, uw, dw):
    width, f = inputs.shape[1], gw.shape[1]
    vmem = pl.BlockSpec(memory_space=pltpu.VMEM)
    hbm = pl.BlockSpec(memory_space=pl.ANY)
    dma = pltpu.SemaphoreType.DMA
    n = len(UNITS)
    parts = min(pieces for _, pieces in GROUPS)
    per_group = []
    for slots, pieces in GROUPS:
        r, dc = PEERS * slots, width // pieces
        rows = PLANE * r
        per_group.append([
            ((2, pieces, PLANE, r, dc), BF16),
            ((2, rows, dc), BF16),
            ((rows, 4 * f), F32),
            ((rows, 2 * f), F32),
            ((rows, 2 * f), BF16),
            ((rows, 4 * f), BF16),
            ((2, pieces, PLANE, r, dc), BF16),
            ((2, pieces, 2, 2, r, dc), BF16),
            ((2, pieces, 2, RING, r, dc), BF16),
            ((2, pieces, RING, r, dc), BF16),
            ((2, pieces, 2, r, dc // 2), BF16),
            ((2, pieces, 2, r, dc), BF16),
            ((2 * r, dc), F32),
        ])
    out = jax.ShapeDtypeStruct(inputs.shape, BF16)
    return pl.pallas_call(
        moe_kernel,
        out_shape=(out, out),
        in_specs=[vmem] * 7 + [hbm] * 3,
        out_specs=(vmem, vmem),
        scratch_shapes=[
            pltpu.VMEM((16, width), F32),
            pltpu.VMEM((BLOCK, width), BF16),
            pltpu.VMEM((BLOCK, width), BF16),
            pltpu.VMEM((BLOCK, width), BF16),
            pltpu.VMEM((BLOCK, width), BF16),
            pltpu.VMEM((8, width), BF16),
            pltpu.VMEM((16, PEERS * 8), F32),
            pltpu.VMEM((len(GROUPS), PEERS, BLOCK, width), BF16),
            pltpu.VMEM((len(GROUPS), PEERS, BLOCK, width), BF16),
            pltpu.VMEM((len(GROUPS), PEERS, BLOCK, width), BF16),
            pltpu.VMEM((len(GROUPS), PEERS, BLOCK, width), BF16),
            pltpu.VMEM((4 * f, width), BF16),
            pltpu.VMEM((2 * f, width), BF16),
            *[pltpu.VMEM(*group[i]) for i in range(13) for group in per_group],
            dma((3,)),
            dma((2,)),
            dma((2, parts)),
            dma((n,)),
            dma((n,)),
            dma((n,)),
            dma((n, 2, 2)),
            dma((n,)),
            dma((n, 2, 2)),
            dma((n,)),
            dma((n,)),
        ],
        compiler_params=pltpu.CompilerParams(
            collective_id=0, has_side_effects=True, vmem_limit_bytes=58 << 20
        ),
    )(inputs, conv, ids, gate_values, cot, sel, ret, gw, uw, dw)


def row_maps():
    sel = []
    ret = np.zeros((len(GROUPS), PEERS * 8, 2 * PEERS * GROUPS[0][0]), ml_dtypes.bfloat16)
    for g, (slots, _) in enumerate(GROUPS):
        r = PEERS * slots
        m = np.zeros((2 * r, PEERS * 8), ml_dtypes.bfloat16)
        for a in range(2):
            for s in range(PEERS):
                for i in range(slots):
                    m[a * r + s * slots + i, s * 8 + a * slots + i] = 1
        sel.append(m)
        ret[g, :, : 2 * r] = m.T
    return jnp.asarray(np.concatenate(sel)), jnp.asarray(ret.reshape(-1, ret.shape[-1]))


def per_device(
    inputs, conv_weight, expert_ids, gate_values, cotangent, gate_weight, up_weight, down_weight
):
    sel, ret = row_maps()
    return moe(
        inputs, conv_weight, expert_ids.T, gate_values.T, cotangent, sel, ret,
        jnp.swapaxes(gate_weight, 1, 2), jnp.swapaxes(up_weight, 1, 2), down_weight,
    )


def solution(mesh):
    in_specs = (
        P(("exp", "tp"), None),
        P(),
        P(("exp", "tp"), None),
        P(("exp", "tp"), None),
        P(("exp", "tp"), None),
        P("exp", None, "tp"),
        P("exp", None, "tp"),
        P("exp", "tp", None),
    )
    out_specs = (P(("exp", "tp"), None), P(("exp", "tp"), None))
    return jax.shard_map(
        per_device, mesh=mesh, in_specs=in_specs, out_specs=out_specs, check_vma=False
    )
```

time: 405 us -> 115 us (0.28)
  waiting for transfers between devices: 208 us -> 0 us
  Pallas kernels: 0 us -> 111 us
  local copies, waits for them, and re-layouts: 76.9 us -> 2.95 us
  matrix products: 54.2 us -> 0 us
  other arithmetic: 24.4 us -> 0 us
  starting transfers between devices: 16.7 us -> 0 us
  between operations: 14.3 us -> 0.64 us
  blocking collectives: 7.82 us -> 0 us
    psum x1 -> x0, waiting for transfers between devices: 132 us -> none  [per_device(): summed = lax.psum(partials, 'tp').astype(jnp.float32)]
    pallas_call x0 -> x1, Pallas kernels: none -> 111 us  [moe(): pl.pallas_call(moe_kernel, out_shape=(out, out), in_specs=[vmem] * 7 + [h...]
    all_gather x1 -> x0, waiting for transfers between devices: 64.8 us -> none  [per_device(): piece = lax.all_gather(stacked, 'tp', axis=0, tiled=True)]
    dot_general x8 -> x0, matrix products: 54.2 us -> none  [the longest x1 11.1 us: expert_rows(): jnp.einsum('mjsf,jdf->mjsd', grad_up, up_weight, preferred_element_type=j...]
    another operation x7 -> x0, local copies, waits for them, and re-layouts: 46.7 us -> none  [the longest x2 25.7 us: per_device(): jnp.stack([forward_part.astype(jnp.bfloat16).reshape(shape_back), backwar...]
    another operation x3 -> x0, other arithmetic: 18.6 us -> none  [the longest x1 18 us: per_device(): jnp.stack([forward_part.astype(jnp.bfloat16).reshape(shape_back), backwar...]
    slice x7 -> x0, local copies, waits for them, and re-layouts: 14 us -> none  [the longest x1 11.2 us: per_device(): piece[:, 1].reshape(piece_rows * groups, per_group, slot_count, model_width)]
    all_to_all x2 -> x0, waiting for transfers between devices: 10.1 us -> none  [the longest x1 6.99 us: per_device(): lax.all_to_all(own_sums.astype(jnp.bfloat16), 'exp', split_axis=1, concat...]
  transfers between devices with their start and end apart: 6 -> 0, of which waited for: 5 -> 0; matrix products, arithmetic and copies ran while one was open for 2% -> 0% of each run, Pallas kernels for 0% -> 0%
where the time goes in v2:
time: 115 us
  Pallas kernels  111 us (97%)
  local copies, waits for them, and re-layouts  2.95 us (3%)
    pallas_call x1, Pallas kernels, moe(): pl.pallas_call(moe_kernel, out_shape=(out, out), in_specs=[vmem] * 7 + [h...  111 us
    unnamed x2, local copies, waits for them, and re-layouts  2.95 us

profile of v2, /device:TPU:1, one launch (start us, length us, event | category | flops | bytes accessed | tf_op | source)
XLA Modules:
  0.0 114.9 jit_solution(1732887839453663026)
XLA Ops:
  0.6 111.3 %shard_map.113 = (bf16[8,4096]{1,0:T(8,128)(2,1)}, bf16[8,4096]{1,0:T(8,128)(2,1)}) custom-call(bf16[8,4096]{1,0:T(8,128)(2,1)} %inputs.1, f32[4,4096]{1,0:T(4,128)} %conv.1, s32[2,8]{1,0:T(2,128)} %bitcast.6, f32[2,8]{1,0:T(2,128)} %bitcast.7, bf16[8,4096]{1,0:T(8,128)(2,1)} %cot.1, bf16[48,64]{1,0:T(8,128)(2,1)} %constant.4.clone.sel, ...), custom_call_target="tpu_custom_call" | custom-call | tf_op jit(solution)/shard_map/pallas_call | solution.py:420
  111.9 1.5 %copy.14 = bf16[8,4096]{1,0:T(8,128)(2,1)} copy(bf16[8,4096]{1,0:T(8,128)(2,1)} %get-tuple-element.4) | data formatting | bytes 131072
  113.4 1.5 %copy.15 = bf16[8,4096]{1,0:T(8,128)(2,1)} copy(bf16[8,4096]{1,0:T(8,128)(2,1)} %get-tuple-element.5) | data formatting | bytes 131072

commit v3 on v2

--- a/solution.py
+++ b/solution.py
@@ -16,7 +16,8 @@
 PEERS = 8
 BLOCK = 4
 TAPS = 4
-GROUPS = ((2, 4), (1, 2))
+TILE = 1024
+GROUPS = ((2, 2), (1, 2))
 UNITS = [(g, k) for g, (_, pieces) in enumerate(GROUPS) for k in range(pieces)]
 NT = (((1,), (1,)), ((), ()))
 
@@ -26,7 +27,7 @@
     ext, halo_out, halo_in, back_out, back_in, mixed, gates, pk, xr, pk2, yr, wgu, wd, *rest,
 ):
     per_group, sems = rest[: 13 * len(GROUPS)], rest[13 * len(GROUPS) :]
-    buf, lhs, acc_gu, acc_b, hid, gg, res, rel, ful, part, rel2, ful2, fin = (
+    buf, lhs, acc_gu, acc_b, turned, act, res, rel, ful, part, rel2, ful2, fin = (
         per_group[i * len(GROUPS) : (i + 1) * len(GROUPS)] for i in range(13)
     )
     w_sem, h_sem, b_sem, x_send, x_recv, g_send, g_recv, r_send, r_recv, y_send, y_recv = sems
@@ -186,56 +187,62 @@
             v = jnp.stack([buf[g][1, k, j * RING + s] for j in range(RING)], 0).astype(F32)
             lhs[g][1, s * slab : (s + 1) * slab] = v.reshape(slab, dc).astype(BF16)
 
-        def add(acc, a, w, at, n):
-            made = lax.dot_general(
-                lhs[g][a], w[pl.ds(at, n), cols], NT, preferred_element_type=F32
-            )
-            acc[:, pl.ds(at, n)] = made if k == 0 else acc[:, pl.ds(at, n)] + made
+        def add(acc, a, w, i):
+            r = pl.ds(pl.multiple_of(i * 2 * f, 16), 2 * f)
+            made = lax.dot_general(w[r, cols], lhs[g][a], NT, preferred_element_type=F32)
+            acc[r, :] = made if k == 0 else acc[r, :] + made
 
         def tile(i, carry):
-            add(acc_gu[g], 0, wgu, pl.multiple_of(i * 256, 256), 256)
+            add(acc_gu[g], 0, wgu, i)
             return carry
 
-        lax.fori_loop(0, 4 * f // 256, tile, 0)
-
         def tile_b(i, carry):
-            add(acc_b[g], 1, wd, pl.multiple_of(i * 256, 256), 256)
+            add(acc_b[g], 1, wd, i)
             return carry
 
-        lax.fori_loop(0, 2 * f // 256, tile_b, 0)
-        if 2 * f % 256:
-            add(acc_b[g], 1, wd, 2 * f // 256 * 256, 2 * f % 256)
+        lax.fori_loop(0, 2, tile, 0)
+        tile_b(0, 0)
 
     def activate(g):
+        m = PLANE * rows_of(g)
+
         def strip(i, carry):
-            r = pl.ds(pl.multiple_of(i * 16, 16), 16)
-            gate_pre, up_pre = acc_gu[g][r, : 2 * f], acc_gu[g][r, 2 * f :]
+            at = pl.multiple_of(i * 64, 64)
+            r = pl.ds(at, 64)
+            gate_pre, up_pre = acc_gu[g][r, :], acc_gu[g][pl.ds(2 * f + at, 64), :]
             back = acc_b[g][r, :]
             s = jax.nn.sigmoid(gate_pre)
             silu = gate_pre * s
-            hid[g][r, :] = (silu * up_pre).astype(BF16)
-            gg[g][r, : 2 * f] = (back * up_pre * s * (1.0 + gate_pre * (1.0 - s))).astype(BF16)
-            gg[g][r, 2 * f :] = (back * silu).astype(BF16)
+            turned[g][r, :] = (silu * up_pre).astype(BF16)
+            grad_gate = back * up_pre * s * (1.0 + gate_pre * (1.0 - s))
+            turned[g][pl.ds(2 * f + at, 64), :] = grad_gate.astype(BF16)
+            turned[g][pl.ds(4 * f + at, 64), :] = (back * silu).astype(BF16)
             return carry
 
-        lax.fori_loop(0, PLANE * rows_of(g) // 16, strip, 0)
+        lax.fori_loop(0, 2 * f // 64, strip, 0)
+        one = lax.broadcasted_iota(jnp.int32, (m, m), 0) == lax.broadcasted_iota(jnp.int32, (m, m), 1)
+        one = one.astype(F32).astype(BF16)
+        for i in range(3):
+            r = slice(2 * f * i, 2 * f * (i + 1))
+            back = lax.dot_general(one, turned[g][r, :], NT, preferred_element_type=F32)
+            act[g][:, r] = back.astype(BF16)
 
     def outputs(u):
         g, k = UNITS[u]
         n, dc = rows_of(g), width // GROUPS[g][1]
 
         def tile(i, carry):
-            at = pl.multiple_of(i * 256, 256)
-            cols, to = pl.ds(k * dc + at, 256), pl.ds(at, 256)
-            forward = jnp.dot(hid[g][...], wd[:, cols], preferred_element_type=F32)
-            res[g][0, k, :, :, to] = forward.reshape(PLANE, n, 256).astype(BF16)
-            backward = jnp.dot(gg[g][...], wgu[:, cols], preferred_element_type=F32)
-            backward = backward.reshape(RING, RING, n, 256).astype(BF16)
+            at = pl.multiple_of(i * TILE, TILE)
+            cols, to = pl.ds(k * dc + at, TILE), pl.ds(at, TILE)
+            forward = jnp.dot(act[g][:, : 2 * f], wd[:, cols], preferred_element_type=F32)
+            res[g][0, k, :, :, to] = forward.reshape(PLANE, n, TILE).astype(BF16)
+            backward = jnp.dot(act[g][:, 2 * f :], wgu[:, cols], preferred_element_type=F32)
+            backward = backward.reshape(RING, RING, n, TILE).astype(BF16)
             for s in range(RING):
                 res[g][1, k, s * RING : (s + 1) * RING, :, to] = backward[:, s]
             return carry
 
-        lax.fori_loop(0, dc // 256, tile, 0)
+        lax.fori_loop(0, dc // TILE, tile, 0)
 
     def partial(a, u, phase, j, h=None):
         g, k = UNITS[u]
@@ -256,6 +263,15 @@
                     partial(a, u, phase, (own + 2) % RING, h), (rel, rel2)[phase][g].at[a, k, h],
                     r_send.at[u], r_recv.at[u, phase, 0], to(by),
                 )
+        if phase == 0:
+            for a in range(2):
+                own, to = axes[a][1], steps[a][1]
+                for h, by in ((0, 1), (1, -1)):
+                    remote(
+                        partial(a, u, 0, (own + by) % RING, 1 - h),
+                        ful[g].at[a, k, h, pl.ds(2 * (1 - h), 2)],
+                        r_send.at[u], r_recv.at[u, 0, 1], to(by),
+                    )
 
     def reduce_send(u, phase):
         g, k = UNITS[u]
@@ -266,8 +282,9 @@
                 j = (own + by) % RING
                 mine, came = partial(a, u, phase, j, h), (rel, rel2)[phase][g]
                 mine[...] = (mine[...].astype(F32) + came[a, k, h].astype(F32)).astype(BF16)
+                into = ful[g].at[a, k, h, pl.ds(2 * h, 2)] if phase == 0 else ful2[g].at[a, k, h]
                 remote(
-                    partial(a, u, phase, j), (ful, ful2)[phase][g].at[a, k, h],
+                    mine if phase == 0 else partial(a, u, phase, j), into,
                     r_send.at[u], r_recv.at[u, phase, 1], to(by),
                 )
 
@@ -334,11 +351,11 @@
             gather_send(s, 0)
         if 0 <= s - 1 < n:
             gather_relay(s - 1, 0)
-        if 0 <= s - 4 < n:
-            gather_relay(s - 4, 1)
         if 0 <= s - 2 < n:
             gather_wait(s - 2, 0)
             gather_send(s - 2, 1)
+        if 0 <= s - 3 < n:
+            gather_relay(s - 3, 1)
 
     def gather_end(u):
         if u == 0:
@@ -365,14 +382,14 @@
             reduce_sum(s - 4, 1)
             give_back(s - 4)
 
-    for s in range(last + 6):
+    for s in range(last + 5):
         gather_step(s)
-        if s >= 5:
-            gather_end(s - 5)
+        if s >= 4:
+            gather_end(s - 4)
     for s in range(n + 4):
         reduce_step(s)
-        if last + 6 + s < n + 5:
-            gather_step(last + 6 + s)
+        if last + 5 + s < n + 4:
+            gather_step(last + 5 + s)
             gather_end(last + 1 + s)
     for i in range(parts):
         combine(i)
@@ -404,10 +421,10 @@
         per_group.append([
             ((2, pieces, PLANE, r, dc), BF16),
             ((2, rows, dc), BF16),
-            ((rows, 4 * f), F32),
-            ((rows, 2 * f), F32),
-            ((rows, 2 * f), BF16),
-            ((rows, 4 * f), BF16),
+            ((4 * f, rows), F32),
+            ((2 * f, rows), F32),
+            ((6 * f, rows), BF16),
+            ((rows, 6 * f), BF16),
             ((2, pieces, PLANE, r, dc), BF16),
             ((2, pieces, 2, 2, r, dc), BF16),
             ((2, pieces, 2, RING, r, dc), BF16),

time: 115 us -> 108 us (0.939)
  Pallas kernels: 111 us -> 104 us
    pallas_call x1, Pallas kernels: 111 us -> 104 us  [moe(): pl.pallas_call(moe_kernel, out_shape=(out, out), in_specs=[vmem] * 7 + [h...]
where the time goes in v3:
time: 108 us
  Pallas kernels  104 us (96%)
  local copies, waits for them, and re-layouts  2.95 us (3%)
    pallas_call x1, Pallas kernels, moe(): pl.pallas_call(moe_kernel, out_shape=(out, out), in_specs=[vmem] * 7 + [h...  104 us
    unnamed x2, local copies, waits for them, and re-layouts  2.95 us

profile of v3, /device:TPU:1, one launch (start us, length us, event | category | flops | bytes accessed | tf_op | source)
XLA Modules:
  0.0 107.8 jit_solution(11789681223984283674)
XLA Ops:
  0.6 104.2 %shard_map.113 = (bf16[8,4096]{1,0:T(8,128)(2,1)}, bf16[8,4096]{1,0:T(8,128)(2,1)}) custom-call(bf16[8,4096]{1,0:T(8,128)(2,1)} %inputs.1, f32[4,4096]{1,0:T(4,128)} %conv.1, s32[2,8]{1,0:T(2,128)} %bitcast.6, f32[2,8]{1,0:T(2,128)} %bitcast.7, bf16[8,4096]{1,0:T(8,128)(2,1)} %cot.1, bf16[48,64]{1,0:T(8,128)(2,1)} %constant.4.clone.sel, ...), custom_call_target="tpu_custom_call" | custom-call | tf_op jit(solution)/shard_map/pallas_call | solution.py:437
  104.8 1.5 %copy.14 = bf16[8,4096]{1,0:T(8,128)(2,1)} copy(bf16[8,4096]{1,0:T(8,128)(2,1)} %get-tuple-element.4) | data formatting | bytes 131072
  106.3 1.5 %copy.15 = bf16[8,4096]{1,0:T(8,128)(2,1)} copy(bf16[8,4096]{1,0:T(8,128)(2,1)} %get-tuple-element.5) | data formatting | bytes 131072

commit v4 on v3

--- a/solution.py
+++ b/solution.py
@@ -17,7 +17,7 @@
 BLOCK = 4
 TAPS = 4
 TILE = 1024
-GROUPS = ((2, 2), (1, 2))
+GROUPS = ((1, 2), (2, 2))
 UNITS = [(g, k) for g, (_, pieces) in enumerate(GROUPS) for k in range(pieces)]
 NT = (((1,), (1,)), ((), ()))
 
@@ -82,7 +82,7 @@
                 peers.append((px * CORES + pc, device(px, z, y, pc)))
     barrier = pltpu.get_barrier_semaphore()
     partners = [to for _, to in peers] + [s(by) for s in steps[0] for by in (1, -1)]
-    partners += [line(1), line(-1)]
+    partners += [line(1), line(-1), step_y(2), step_z(2)]
     for to in partners:
         pl.semaphore_signal(barrier, inc=1, device_id=to, device_id_type=MESH)
 
@@ -96,8 +96,8 @@
     named = [(expert == ids[k : k + 1, :]).astype(F32) for k in range(2)]
     earlier = jnp.dot(named[0] + named[1], before.astype(F32), preferred_element_type=F32)
     at = [
-        jnp.where(row == 4, 2, jnp.where(row < 2, row, -1)),
-        jnp.where(row == 5, 2, jnp.where((row == 2) | (row == 3), row - 2, -1)),
+        jnp.where(row == 0, 0, jnp.where((row == 4) | (row == 5), row - 3, -1)),
+        jnp.where(row == 1, 0, jnp.where(row > 5, row - 5, -1)),
     ]
     hit = [(earlier == at[a].astype(F32)).astype(F32) for a in range(2)]
     disp = [((named[0] + named[1]) * hit[a]).astype(BF16) for a in range(2)]
@@ -111,14 +111,14 @@
 
     pl.semaphore_wait(barrier, len(partners))
     remote(halo_out, halo_in, h_sem.at[0], h_sem.at[1], line(1))
+    packed = jnp.dot(disp[1], cot[...], preferred_element_type=F32)
     wait(h_sem.at[1], halo_in)
     ext[4:8, :] = jnp.where(here == 0, 0.0, halo_in[...].astype(F32))
     total = own
     for j in range(TAPS):
         total = total + conv[j : j + 1, :] * ext[8 - j : 16 - j, :]
     mixed[...] = total.astype(BF16)
-    packed = jnp.dot(disp[0], mixed[...], preferred_element_type=F32)
-    packed = packed + jnp.dot(disp[1], cot[...], preferred_element_type=F32)
+    packed = packed + jnp.dot(disp[0], mixed[...], preferred_element_type=F32)
     packed = packed.reshape(PEERS, 8, width)
     pk[0] = packed[:, :BLOCK].astype(BF16)
     pk[1] = packed[:, BLOCK:].astype(BF16)
@@ -149,14 +149,24 @@
         g, k = UNITS[u]
         return buf[g].at[0, k, pl.ds(0, n)]
 
+    def direct_gather(u, phase):
+        return phase == 0 and u < 1
+
+    def direct_reduce(u, phase):
+        return phase == 1 and u == len(UNITS) - 1
+
     def gather_send(u, phase):
         for a in range(2):
             v = gather_view(a, u, phase, axes[a][phase])
             for by in (1, -1):
                 remote(v, v, g_send.at[u], g_recv.at[u, phase, 0], steps[a][phase](by))
+            if direct_gather(u, phase):
+                remote(v, v, g_send.at[u], g_recv.at[u, phase, 1], steps[a][phase](2))
 
     def gather_relay(u, phase):
         wait(g_recv.at[u, phase, 0], blocks(u, (4, 16)[phase]))
+        if direct_gather(u, phase):
+            return
         for a in range(2):
             for h, by in ((0, 1), (1, -1)):
                 v = gather_view(a, u, phase, (axes[a][phase] - by) % RING, h)
@@ -258,11 +268,17 @@
         g, k = UNITS[u]
         for a in range(2):
             own, to = axes[a][1 - phase], steps[a][1 - phase]
+            far = direct_reduce(u, phase)
             for h, by in ((0, 1), (1, -1)):
                 remote(
                     partial(a, u, phase, (own + 2) % RING, h), (rel, rel2)[phase][g].at[a, k, h],
-                    r_send.at[u], r_recv.at[u, phase, 0], to(by),
+                    r_send.at[u], r_recv.at[u, phase, 0], to(2 if far else by),
                 )
+                if far:
+                    remote(
+                        partial(a, u, phase, (own + by) % RING), ful2[g].at[a, k, h],
+                        r_send.at[u], r_recv.at[u, phase, 1], to(by),
+                    )
         if phase == 0:
             for a in range(2):
                 own, to = axes[a][1], steps[a][1]
@@ -275,6 +291,8 @@
 
     def reduce_send(u, phase):
         g, k = UNITS[u]
+        if direct_reduce(u, phase):
+            return
         wait(r_recv.at[u, phase, 0], blocks(u, (8, 2)[phase]))
         for a in range(2):
             own, to = axes[a][1 - phase], steps[a][1 - phase]
@@ -292,10 +310,15 @@
         g, k = UNITS[u]
         n = rows_of(g)
         wait(r_recv.at[u, phase, 1], blocks(u, (16, 4)[phase]))
+        if direct_reduce(u, phase):
+            wait(r_recv.at[u, phase, 0], blocks(u, 2))
         for a in range(2):
             came = (ful, ful2)[phase][g]
             total = partial(a, u, phase, axes[a][1 - phase])[...].astype(F32)
             total = total + came[a, k, 0].astype(F32) + came[a, k, 1].astype(F32)
+            if direct_reduce(u, phase):
+                far = [rel2[g][a, k, h].astype(F32) for h in range(2)]
+                total = total + jnp.concatenate(far, 1)
             if phase == 0:
                 part[g][a, k] = total.astype(BF16)
             else:
@@ -474,7 +497,8 @@
 
 def row_maps():
     sel = []
-    ret = np.zeros((len(GROUPS), PEERS * 8, 2 * PEERS * GROUPS[0][0]), ml_dtypes.bfloat16)
+    most = max(slots for slots, _ in GROUPS)
+    ret = np.zeros((len(GROUPS), PEERS * 8, 2 * PEERS * most), ml_dtypes.bfloat16)
     for g, (slots, _) in enumerate(GROUPS):
         r = PEERS * slots
         m = np.zeros((2 * r, PEERS * 8), ml_dtypes.bfloat16)

time: 108 us -> 106 us (0.981)
  Pallas kernels: 104 us -> 102 us
    pallas_call x1, Pallas kernels: 104 us -> 102 us  [moe(): pl.pallas_call(moe_kernel, out_shape=(out, out), in_specs=[vmem] * 7 + [h...]
where the time goes in v4:
time: 106 us
  Pallas kernels  102 us (96%)
  local copies, waits for them, and re-layouts  2.95 us (3%)
    pallas_call x1, Pallas kernels, moe(): pl.pallas_call(moe_kernel, out_shape=(out, out), in_specs=[vmem] * 7 + [h...  102 us
    unnamed x2, local copies, waits for them, and re-layouts  2.95 us

profile of v4, /device:TPU:1, one launch (start us, length us, event | category | flops | bytes accessed | tf_op | source)
XLA Modules:
  0.0 105.8 jit_solution(17354955243623994241)
XLA Ops:
  0.6 102.2 %shard_map.113 = (bf16[8,4096]{1,0:T(8,128)(2,1)}, bf16[8,4096]{1,0:T(8,128)(2,1)}) custom-call(bf16[8,4096]{1,0:T(8,128)(2,1)} %inputs.1, f32[4,4096]{1,0:T(4,128)} %conv.1, s32[2,8]{1,0:T(2,128)} %bitcast.6, f32[2,8]{1,0:T(2,128)} %bitcast.7, bf16[8,4096]{1,0:T(8,128)(2,1)} %cot.1, bf16[48,64]{1,0:T(8,128)(2,1)} %constant.4.clone.sel, ...), custom_call_target="tpu_custom_call" | custom-call | tf_op jit(solution)/shard_map/pallas_call | solution.py:460
  102.8 1.5 %copy.14 = bf16[8,4096]{1,0:T(8,128)(2,1)} copy(bf16[8,4096]{1,0:T(8,128)(2,1)} %get-tuple-element.4) | data formatting | bytes 131072
  104.3 1.5 %copy.15 = bf16[8,4096]{1,0:T(8,128)(2,1)} copy(bf16[8,4096]{1,0:T(8,128)(2,1)} %get-tuple-element.5) | data formatting | bytes 131072

commit v5 on v4

--- a/solution.py
+++ b/solution.py
@@ -86,6 +86,10 @@
     for to in partners:
         pl.semaphore_signal(barrier, inc=1, device_id=to, device_id_type=MESH)
 
+    weights = ((gw, wgu, 0), (uw, wgu, 2 * f), (dw, wd, 0))
+    for w, into, first in weights:
+        pltpu.make_async_copy(w.at[c], into.at[pl.ds(first, f)], w_sem.at[0]).start()
+
     own = inputs[...].astype(F32)
     ext[8:16, :] = own
     halo_out[...] = own[4:8].astype(BF16)
@@ -102,13 +106,6 @@
     hit = [(earlier == at[a].astype(F32)).astype(F32) for a in range(2)]
     disp = [((named[0] + named[1]) * hit[a]).astype(BF16) for a in range(2)]
     gate = named[0] * gate_values[0:1, :] + named[1] * gate_values[1:2, :]
-    same = lax.broadcasted_iota(jnp.int32, (8, 8), 0) == lax.broadcasted_iota(jnp.int32, (8, 8), 1)
-    for a in range(2):
-        gates[a * 8 : (a + 1) * 8, :] = lax.dot_general(
-            same.astype(F32), gate * hit[a], NT,
-            preferred_element_type=F32, precision=lax.Precision.HIGHEST,
-        )
-
     pl.semaphore_wait(barrier, len(partners))
     remote(halo_out, halo_in, h_sem.at[0], h_sem.at[1], line(1))
     packed = jnp.dot(disp[1], cot[...], preferred_element_type=F32)
@@ -131,10 +128,16 @@
         xr[g, q] = pk[g, q]
 
     sibling = device(x, z, y, 1 - c)
-    for w, into, first in ((gw, wgu, 0), (uw, wgu, 2 * f), (dw, wd, 0)):
-        pltpu.make_async_copy(w.at[c], into.at[pl.ds(first, f)], w_sem.at[0]).start()
+    for w, into, first in weights:
         remote(
             w.at[1 - c], into.at[pl.ds(first + f, f)], w_sem.at[1], w_sem.at[2], sibling
+        )
+
+    same = lax.broadcasted_iota(jnp.int32, (8, 8), 0) == lax.broadcasted_iota(jnp.int32, (8, 8), 1)
+    for a in range(2):
+        gates[a * 8 : (a + 1) * 8, :] = lax.dot_general(
+            same.astype(F32), gate * hit[a], NT,
+            preferred_element_type=F32, precision=lax.Precision.HIGHEST,
         )
 
     def gather_view(a, u, phase, j, h=None):

time: 106 us -> 106 us (level)
  no operation moved by 1% of the time
where the time goes in v5:
time: 106 us
  Pallas kernels  102 us (96%)
  local copies, waits for them, and re-layouts  2.95 us (3%)
    pallas_call x1, Pallas kernels, moe(): pl.pallas_call(moe_kernel, out_shape=(out, out), in_specs=[vmem] * 7 + [h...  102 us
    unnamed x2, local copies, waits for them, and re-layouts  2.95 us

profile of v5, /device:TPU:1, one launch (start us, length us, event | category | flops | bytes accessed | tf_op | source)
XLA Modules:
  0.0 105.8 jit_solution(10088312304226206718)
XLA Ops:
  0.6 102.2 %shard_map.113 = (bf16[8,4096]{1,0:T(8,128)(2,1)}, bf16[8,4096]{1,0:T(8,128)(2,1)}) custom-call(bf16[8,4096]{1,0:T(8,128)(2,1)} %inputs.1, f32[4,4096]{1,0:T(4,128)} %conv.1, s32[2,8]{1,0:T(2,128)} %bitcast.6, f32[2,8]{1,0:T(2,128)} %bitcast.7, bf16[8,4096]{1,0:T(8,128)(2,1)} %cot.1, bf16[48,64]{1,0:T(8,128)(2,1)} %constant.4.clone.sel, ...), custom_call_target="tpu_custom_call" | custom-call | tf_op jit(solution)/shard_map/pallas_call | solution.py:463
  102.8 1.5 %copy.14 = bf16[8,4096]{1,0:T(8,128)(2,1)} copy(bf16[8,4096]{1,0:T(8,128)(2,1)} %get-tuple-element.4) | data formatting | bytes 131072
  104.3 1.5 %copy.15 = bf16[8,4096]{1,0:T(8,128)(2,1)} copy(bf16[8,4096]{1,0:T(8,128)(2,1)} %get-tuple-element.5) | data formatting | bytes 131072
